TPU v7x, 32 devices: a whole 2x2x4 slice. The times are simulated.
32 devices in a mesh: section: 16 (over z, y, x), tensor: 2 (over core).
Axes of the slice: x: 2, y: 2, z: 4, core: 2. Of those that a mesh axis runs over, the one named last changes fastest.
Arguments:
- embedded: bfloat16 [256, 4096], P(None, 'tensor'), may hold values from -6 to 6
- outbox: bfloat16 [16, 256, 4096], P('section', None, 'tensor'), may hold values from -6 to 6
- loss_grad: bfloat16 [256, 4096], P(None, 'tensor'), may hold values from -6 to 6
- grad_outbox: bfloat16 [16, 256, 4096], P('section', None, 'tensor'), may hold values from -6 to 6
- stash_held: bfloat16 [16, 256, 4096], P('section', None, 'tensor'), may hold values from -6 to 6
- norm_gain: bfloat16 [16, 4096], P('section', 'tensor'), may hold values from 0.099609375 to 1.8984375
- w_query: bfloat16 [16, 4096, 1024], P('section', None, 'tensor'), may hold values from -4 to 4
- w_keyval: bfloat16 [16, 4096, 512], P('section', None, 'tensor'), may hold values from -1 to 1
- w_out: bfloat16 [16, 1024, 4096], P('section', 'tensor'), may hold values from -0.25 to 0.25
Outputs:
- section_out: bfloat16 [16, 256, 4096], P('section', None, 'tensor')
- evicted: bfloat16 [16, 256, 4096], P('section', None, 'tensor')
- input_grad: bfloat16 [16, 256, 4096], P('section', None, 'tensor')
All inputs are finite; a program needn't handle non-finite values.
Results may differ from a plain program's by a relative error of at most 0.013.
Values may be sent and summed in bfloat16 or wider, within the bound.
No kernel may reach another device: no remote copies, remote signals or barrier semaphores. Data moves between devices by JAX's collectives and lax.ppermute only.
A program may use at most 64 MiB of HBM per device.

v0:
```python
import functools

import jax
import jax.numpy as jnp
from jax import lax
from jax.experimental import pallas as pl
from jax.experimental.pallas import tpu as pltpu
from jax.sharding import PartitionSpec as P


HEAD = 128
EPS = 1e-05
SCALE = HEAD ** (-0.5)
F32 = jnp.float32
BF16 = jnp.bfloat16

LIMIT = 14 * 2**20


def rotate(value, axis, k):
    count = lax.axis_size(axis)
    return lax.ppermute(value, axis, [(i, (i - k) % count) for i in range(count)])


def gathered(value, axis):
    return [value] + [rotate(value, axis, k) for k in range(1, lax.axis_size(axis))]


def reduced(parts, axis):
    total = parts[0].astype(F32)
    for k in range(1, len(parts)):
        total = total + rotate(parts[k], axis, -k).astype(F32)
    return total


def nt(a, b):
    return lax.dot_general(a, b, (((1,), (1,)), ((), ())), preferred_element_type=F32)


def tn(a, b):
    return lax.dot_general(a, b, (((0,), (0,)), ((), ())), preferred_element_type=F32)


def nn(a, b):
    return jnp.dot(a, b, preferred_element_type=F32)


def vmem_spec():
    return pl.BlockSpec(memory_space=pltpu.VMEM)


def any_spec():
    return pl.BlockSpec(memory_space=pl.ANY)


def rows_of(ref, col, k, count):
    width = ref.shape[0] // count
    return ref[pl.ds(pl.multiple_of(lax.rem(col + k, count) * width, width), width), :]


def columns_of(ref, col, k, count):
    width = ref.shape[1] // count
    return ref[:, pl.ds(pl.multiple_of(lax.rem(col + k, count) * width, width), width)]


def project(normed, weights, col, count):
    width = weights.shape[0] // count
    total = None
    for k in range(count):
        part = nn(normed[:, k * width : (k + 1) * width], rows_of(weights, col, k, count))
        total = part if total is None else total + part
    return total.astype(BF16)


def normalize(xs, gains, normed):
    width = xs[0].shape[1]
    total = None
    for x in xs:
        xf = x[...].astype(F32)
        part = jnp.sum(xf * xf, axis=-1, keepdims=True)
        total = part if total is None else total + part
    inv = lax.rsqrt(total / (width * len(xs)) + EPS)
    for k, x in enumerate(xs):
        xf = x[...].astype(F32)
        normed[:, k * width : (k + 1) * width] = (xf * inv * gains[k][...].astype(F32)).astype(BF16)
    return inv


def causal_mask(seq):
    rows = lax.broadcasted_iota(jnp.int32, (seq, seq), 0)
    cols = lax.broadcasted_iota(jnp.int32, (seq, seq), 1)
    return rows >= cols


def softmax(query, keys, mask):
    scores = jnp.where(mask, nt(query, keys) * SCALE, -1e30)
    top = jnp.max(scores, axis=-1, keepdims=True)
    weights = jnp.exp(scores - top)
    return weights / jnp.sum(weights, axis=-1, keepdims=True)


def forward_kernel(count, heads, *refs):
    xs, refs = refs[:count], refs[count:]
    gains, refs = refs[:count], refs[count:]
    wq, wkv, wo, refs = *refs[:3], refs[3:]
    outs, (normed, attn) = refs[:count], refs[count:]
    col = lax.axis_index("tensor")
    normalize(xs, gains, normed)
    keyval = project(normed, wkv, col, count)
    query = project(normed, wq, col, count)
    keys, values = keyval[:, :HEAD], keyval[:, HEAD:]
    mask = causal_mask(query.shape[0])
    for h in range(heads):
        prob = softmax(query[:, h * HEAD : (h + 1) * HEAD], keys, mask)
        attn[:, h * HEAD : (h + 1) * HEAD] = nn(prob.astype(BF16), values).astype(BF16)
    for k in reversed(range(count)):
        outs[k][...] = nn(attn[...], columns_of(wo, col, k, count)).astype(BF16)


def backward_kernel(count, heads, *refs):
    gs, refs = refs[:count], refs[count:]
    xs, refs = refs[:count], refs[count:]
    gains, refs = refs[:count], refs[count:]
    wq, wkv, wo, refs = *refs[:3], refs[3:]
    outs, (total_out, inv_out, normed, query, prob, d_query) = refs[:count], refs[count:]
    col = lax.axis_index("tensor")
    inv = normalize(xs, gains, normed)
    inv_out[...] = jnp.broadcast_to(inv, inv_out.shape)
    keyval = project(normed, wkv, col, count)
    query[...] = project(normed, wq, col, count)
    mask = causal_mask(query.shape[0])
    for h in range(heads):
        prob[h] = softmax(query[:, h * HEAD : (h + 1) * HEAD], keyval[:, :HEAD], mask)
    d_attn = None
    for k in range(count):
        part = nt(gs[k][...], columns_of(wo, col, k, count))
        d_attn = part if d_attn is None else d_attn + part
    d_attn = d_attn.astype(BF16)
    keys, values = keyval[:, :HEAD], keyval[:, HEAD:]
    d_key = d_value = None
    for h in range(heads):
        span = slice(h * HEAD, (h + 1) * HEAD)
        p = prob[h]
        d_head = d_attn[:, span]
        d_prob = nt(d_head, values)
        d_score = p * (d_prob - jnp.sum(p * d_prob, axis=-1, keepdims=True)) * SCALE
        d_score = d_score.astype(BF16)
        d_query[:, span] = nn(d_score, keys).astype(BF16)
        dk = tn(d_score, query[:, span])
        dv = tn(p.astype(BF16), d_head)
        d_key = dk if d_key is None else d_key + dk
        d_value = dv if d_value is None else d_value + dv
    d_pairs = jnp.concatenate([d_key.astype(BF16), d_value.astype(BF16)], axis=1)
    total = None
    for k in reversed(range(count)):
        term = nt(d_query[...], rows_of(wq, col, k, count))
        term = (term + nt(d_pairs, rows_of(wkv, col, k, count))).astype(BF16)
        outs[k][...] = term
        scaled = term.astype(F32) * gains[k][...].astype(F32)
        part = jnp.sum(scaled * xs[k][...].astype(F32), axis=-1, keepdims=True)
        total = part if total is None else total + part
    total_out[...] = jnp.broadcast_to(total, total_out.shape)


def load_kernel(count, heads, *refs):
    half = (len(refs) - 1) // 2
    sems = refs[-1]
    copies = [
        pltpu.make_async_copy(refs[i], refs[half + i], sems.at[i]) for i in range(half)
    ]
    for copy in copies:
        copy.start()
    for copy in copies:
        copy.wait()


def merge_kernel(count, block, relayed, near, far, last, out, sem):
    place, sections = lax.axis_index("section"), lax.axis_size("section")
    ends = (0, block - 1, sections - block - 1, sections - 1, sections)
    for low, high, source in zip(ends, ends[1:], (relayed, near, far, last)):

        @pl.when((place >= low) & (place < high))
        def _():
            copy = pltpu.make_async_copy(source, out, sem)
            copy.start()
            copy.wait()


def call(kernel, count, heads, ins, out_shape, scratch, flops, moved, far_in=0, far_out=0):
    return pl.pallas_call(
        functools.partial(kernel, count, heads),
        out_shape=out_shape,
        in_specs=[any_spec() if far_in else vmem_spec()] * len(ins),
        out_specs=[any_spec() if far_out else vmem_spec()] * len(out_shape),
        scratch_shapes=scratch,
        compiler_params=pltpu.CompilerParams(vmem_limit_bytes=LIMIT),
        cost_estimate=pl.CostEstimate(flops=flops, bytes_accessed=moved, transcendentals=0),
    )(*ins)


def local(
    embedded, outbox, loss_grad, grad_outbox, stash_held, norm_gain, w_query, w_keyval, w_out
):
    sections = lax.axis_size("section")
    count = lax.axis_size("tensor")
    position = lax.axis_index("section")
    held, grads_held, stash_held = outbox[0], grad_outbox[0], stash_held[0]
    seq, width = held.shape
    model = width * count
    wq, wkv, wo = w_query[0], w_keyval[0], w_out[0]
    qcols, kvcols = wq.shape[1], wkv.shape[1]
    heads = qcols // HEAD
    shape = jax.ShapeDtypeStruct

    block = sections // 4
    high = sections - block

    def send(value, pairs):
        return lax.ppermute(value, "section", pairs)

    up = [(s, s + 1) for s in range(sections - 1)]
    crossing = send(held, [(s, t) for s, t in up if t % block == 0])
    fetched = send(stash_held, [(s, sections - 1 - s) for s in range(sections)])
    coming = send(grads_held, [(t, s) for s, t in up])
    inside = send(held, [(s, t) for s, t in up if t % block])
    evicted_near = send(held, [(s, sections - 2 - s) for s in range(block, high)])
    evicted_far = send(held, [(s, sections - 2 - s) for s in range(block)])
    relayed = send(inside, [(s, sections - 1 - s) for s in range(high + 1, sections)])
    gains = gathered(norm_gain, "tensor")

    normed = pltpu.VMEM((seq, model), BF16)
    shares = [shape((seq, width), BF16)] * count
    proj = 2 * seq * model * (qcols + kvcols)
    out_flops = 2 * seq * model * qcols
    moved = 2 * model * (2 * qcols + kvcols)
    wq, wkv, wo = call(
        load_kernel, count, heads, [wq, wkv, wo],
        [shape(w.shape, w.dtype) for w in (wq, wkv, wo)],
        [pltpu.SemaphoreType.DMA((3,))], 0, 2 * moved, far_in=1,
    )
    bs = gathered(fetched, "tensor")
    arrived = jnp.where(position % block == 0, crossing, inside)
    x_shard = jnp.where(position == 0, embedded, arrived)
    xs = gathered(x_shard, "tensor")
    parts = call(
        forward_kernel, count, heads,
        [*xs, *gains, wq, wkv, wo], shares,
        [normed, pltpu.VMEM((seq, qcols), BF16)],
        proj + out_flops, moved,
    )
    mixed = reduced(parts, "tensor")
    section_out = (x_shard.astype(F32) + mixed).astype(BF16)

    g_shard = jnp.where(position == sections - 1, loss_grad, coming)
    gs = gathered(g_shard, "tensor")
    *terms, total, inv = call(
        backward_kernel, count, heads,
        [*gs, *bs, *gains, wq, wkv, wo],
        [*shares, shape((seq, HEAD), F32), shape((seq, HEAD), F32)],
        [
            normed,
            pltpu.VMEM((seq, qcols), BF16),
            pltpu.VMEM((heads, seq, seq), F32),
            pltpu.VMEM((seq, qcols), BF16),
        ],
        2 * proj + out_flops, moved,
    )
    d_normed = reduced(terms, "tensor")
    total = sum(gathered(total, "tensor"))[:, :1]
    inv = inv[:, :1]
    scaled = d_normed * norm_gain.astype(F32)
    result = (
        g_shard.astype(F32) + inv * scaled - fetched.astype(F32) * inv**3 * (total / model)
    ).astype(BF16)
    last, _ = lax.optimization_barrier((embedded, (result, section_out)))
    (evicted,) = call(
        merge_kernel, count, block,
        [relayed, evicted_near, evicted_far, last], [shape((seq, width), BF16)],
        [pltpu.SemaphoreType.DMA], 0, 4 * seq * width, far_out=1,
    )
    return section_out[None], evicted[None], result[None]


def solution(mesh):
    return jax.shard_map(
        local,
        mesh=mesh,
        in_specs=(
            P(None, "tensor"),
            P("section", None, "tensor"),
            P(None, "tensor"),
            P("section", None, "tensor"),
            P("section", None, "tensor"),
            P("section", "tensor"),
            P("section", None, "tensor"),
            P("section", None, "tensor"),
            P("section", "tensor", None),
        ),
        out_specs=(
            P("section", None, "tensor"),
            P("section", None, "tensor"),
            P("section", None, "tensor"),
        ),
        check_vma=False,
    )
```

profile of v0, /device:TPU:17, one launch (start us, length us, event | category | flops | bytes accessed | tf_op | source)
XLA Modules:
  0.0 149.2 jit_solution(2531594916326277212)
XLA Ops:
  0.6 3.2 %collective-permute-start.1 = (bf16[256,2048]{1,0:T(8,128)(2,1)}, bf16[256,2048]{1,0:T(8,128)(2,1)S(1)}, u32[]{:S(2)}, u32[]{:S(2)}) collective-permute-start(bf16[256,2048]{1,0:T(8,128)(2,1)} %bitcast.19), channel_id=1, source_target_pairs={{0,2},{2,4},{4,6},{8,10},{10,12},{12,14},{16,18},{18,20},{20,22},{... | collective-permute-start | bytes 3145736 | tf_op jit(solution)/shard_map/ppermute | solution.py:219
  3.8 1.3 collective-permute-start
  5.1 5.9 %collective-permute-start.8 = (bf16[256,2048]{1,0:T(8,128)(2,1)}, bf16[256,2048]{1,0:T(8,128)(2,1)}, u32[]{:S(2)}, u32[]{:S(2)}) collective-permute-start(bf16[256,2048]{1,0:T(8,128)(2,1)} %bitcast.17), channel_id=1, source_target_pairs={{2,0},{4,2},{6,4},{8,6},{10,8},{12,10},{14,12},{16,14},{18,16},{20... | collective-permute-start | bytes 3145736 | tf_op jit(solution)/shard_map/ppermute | solution.py:219
  11.1 59.8 %collective-permute-done.1 = bf16[256,2048]{1,0:T(8,128)(2,1)S(1)} collective-permute-done((bf16[256,2048]{1,0:T(8,128)(2,1)}, bf16[256,2048]{1,0:T(8,128)(2,1)S(1)}, u32[]{:S(2)}, u32[]{:S(2)}) %collective-permute-start.1) | collective-permute-done | bytes 1048608 | tf_op jit(solution)/shard_map/ppermute | solution.py:219
  71.0 1.6 %collective-permute-start.2 = (bf16[256,2048]{1,0:T(8,128)(2,1)S(1)}, bf16[256,2048]{1,0:T(8,128)(2,1)S(1)}, u32[]{:S(2)}, u32[]{:S(2)}) collective-permute-start(bf16[256,2048]{1,0:T(8,128)(2,1)S(1)} %select_select_fusion.refs_0_), channel_id=1, source_target_pairs={{0,1},{1,0},{2,3},{3,2},{4,5},{5,4},{6,7},{7,6},{8,9},{9,8},{10,11... | collective-permute-start | bytes 3145736 | tf_op jit(solution)/shard_map/ppermute | solution.py:22
  72.6 0.2 collective-permute-done.8
  72.8 1.3 broadcast_select_fusion.refs_0_
  74.1 1.6 %collective-permute-start.9 = (bf16[256,2048]{1,0:T(8,128)(2,1)S(1)}, bf16[256,2048]{1,0:T(8,128)(2,1)S(1)}, u32[]{:S(2)}, u32[]{:S(2)}) collective-permute-start(bf16[256,2048]{1,0:T(8,128)(2,1)S(1)} %broadcast_select_fusion.refs_0_), channel_id=1, source_target_pairs={{0,1},{1,0},{2,3},{3,2},{4,5},{5,4},{6,7},{7,6},{8,9},{9,8},{10,11... | collective-permute-start | bytes 3145736 | tf_op jit(solution)/shard_map/ppermute | solution.py:22
  75.7 1.9 %collective-permute-done.10.refs_2_ = bf16[256,2048]{1,0:T(8,128)(2,1)S(1)} collective-permute-done((bf16[256,2048]{1,0:T(8,128)(2,1)}, bf16[256,2048]{1,0:T(8,128)(2,1)S(1)}, u32[]{:S(2)}, u32[]{:S(2)}) %collective-permute-start.10) | collective-permute-done | bytes 1048608 | tf_op jit(solution)/shard_map/ppermute | solution.py:219
  77.6 2.0 %collective-permute-start.11 = (bf16[256,2048]{1,0:T(8,128)(2,1)S(1)}, bf16[256,2048]{1,0:T(8,128)(2,1)S(1)}, u32[]{:S(2)}, u32[]{:S(2)}) collective-permute-start(bf16[256,2048]{1,0:T(8,128)(2,1)S(1)} %collective-permute-done.10.refs_2_), channel_id=1, source_target_pairs={{0,1},{1,0},{2,3},{3,2},{4,5},{5,4},{6,7},{7,6},{8,9},{9,8},{10,11... | collective-permute-start | bytes 3145736 | tf_op jit(solution)/shard_map/ppermute | solution.py:22
  79.7 2.2 %copy-done.2 = bf16[1,512,4096]{2,1,0:T(8,128)(2,1)S(1)} copy-done((bf16[1,512,4096]{2,1,0:T(8,128)(2,1)S(1)}, bf16[1,512,4096]{2,1,0:T(8,128)(2,1)}, u32[]{:S(2)}) %copy-start.2) | copy-done | bytes 4194328
  81.9 0.7 shard_map.112
  82.6 5.3 %shard_map.113 = (bf16[256,2048]{1,0:T(8,128)(2,1)S(1)}, bf16[256,2048]{1,0:T(8,128)(2,1)S(1)}) custom-call(bf16[256,2048]{1,0:T(8,128)(2,1)S(1)} %select_select_fusion.refs_0_, bf16[256,2048]{1,0:T(8,128)(2,1)S(1)} %collective-permute-done.2.refs_1_, bf16[1,2048]{1,0:T(2,128)(2,1)S(1)} %copy-done.4, ...), custom_call_target="tpu_custom_call" | custom-call | flops 2684354560 | bytes 10485760 | tf_op jit(solution)/shard_map/pallas_call | solution.py:190
  87.9 0.6 collective-permute-start.4
  88.5 9.3 %shard_map.114 = (bf16[256,2048]{1,0:T(8,128)(2,1)S(1)}, bf16[256,2048]{1,0:T(8,128)(2,1)S(1)}, f32[256,128]{1,0:T(8,128)S(1)}, f32[256,128]{1,0:T(8,128)S(1)}) custom-call(bf16[256,2048]{1,0:T(8,128)(2,1)S(1)} %broadcast_select_fusion.refs_0_, bf16[256,2048]{1,0:T(8,128)(2,1)S(1)} %collective-permute-done.9.refs_1_, ...), custom_call_target="tpu_custom_call" | custom-call | flops 4294967296 | bytes 10485760 | tf_op jit(solution)/shard_map/pallas_call | solution.py:190
  97.9 0.5 collective-permute-start.13
  98.3 2.9 %collective-permute-start.6 = (bf16[256,2048]{1,0:T(8,128)(2,1)S(1)}, bf16[256,2048]{1,0:T(8,128)(2,1)S(1)}, u32[]{:S(2)}, u32[]{:S(2)}) collective-permute-start(bf16[256,2048]{1,0:T(8,128)(2,1)S(1)} %bitcast.21), channel_id=1, source_target_pairs={{8,20},{10,18},{12,16},{14,14},{16,12},{18,10},{20,8},{22,6},{9,21... | collective-permute-start | bytes 3145736 | tf_op jit(solution)/shard_map/ppermute | solution.py:219
  101.2 0.7 collective-permute-start.7
  102.0 0.1 slice_reduce_fusion
  102.2 0.7 collective-permute-start.5
  103.0 1.5 %add_convert_fusion = bf16[256,2048]{1,0:T(8,128)(2,1)} fusion(bf16[256,2048]{1,0:T(8,128)(2,1)S(1)} %collective-permute-done.4, bf16[256,2048]{1,0:T(8,128)(2,1)S(1)} %get-tuple-element.16, bf16[256,2048]{1,0:T(8,128)(2,1)S(1)} %select_select_fusion.refs_0_), kind=kLoop, calls=%fused_computation.1 | loop fusion | flops 3145728 | bytes 4194304 | tf_op jit(solution)/shard_map/convert_element_type | solution.py:252
  104.5 1.9 %subtract_convert_fusion = bf16[256,2048]{1,0:T(8,128)(2,1)} fusion(bf16[256,2048]{1,0:T(8,128)(2,1)S(1)} %collective-permute-done.10.refs_2_, bf16[256,2048]{1,0:T(8,128)(2,1)S(1)} %collective-permute-done.12, bf16[256,2048]{1,0:T(8,128)(2,1)S(1)} %get-tuple-element.19, bf16[256,2048]{1,0:T(8,128)(2,1)S(1)} %broadcast_select_fusion.refs_0_, f32[256]{0:T(256)S(1)} %fusion.2, ...), kind=kLoop, calls=%fused_computation | loop fusion | flops 6291456 | bytes 5254144 | tf_op jit(solution)/shard_map/convert_element_type | solution.py:274
  106.4 41.8 %collective-permute-done.6.near = bf16[256,2048]{1,0:T(8,128)(2,1)S(1)} collective-permute-done((bf16[256,2048]{1,0:T(8,128)(2,1)S(1)}, bf16[256,2048]{1,0:T(8,128)(2,1)S(1)}, u32[]{:S(2)}, u32[]{:S(2)}) %collective-permute-start.6) | collective-permute-done | bytes 1048608 | tf_op jit(solution)/shard_map/ppermute | solution.py:219
  148.2 1.0 shard_map.115
  (27 shorter events, 0.5 us)
Async XLA Ops:
  0.6 70.2 %collective-permute-start.1 = (bf16[256,2048]{1,0:T(8,128)(2,1)}, bf16[256,2048]{1,0:T(8,128)(2,1)S(1)}, u32[]{:S(2)}, u32[]{:S(2)}) collective-permute-start(bf16[256,2048]{1,0:T(8,128)(2,1)} %bitcast.19), channel_id=1, source_target_pairs={{0,2},{2,4},{4,6},{8,10},{10,12},{12,14},{16,18},{18,20},{20,22},{... | collective-permute-start | bytes 3145736 | tf_op jit(solution)/shard_map/ppermute | solution.py:219
  3.8 67.0 %collective-permute-start = (bf16[256,2048]{1,0:T(8,128)(2,1)}, bf16[256,2048]{1,0:T(8,128)(2,1)S(1)}, u32[]{:S(2)}, u32[]{:S(2)}) collective-permute-start(bf16[256,2048]{1,0:T(8,128)(2,1)} %bitcast.20), channel_id=1, source_target_pairs={{6,8},{14,16},{22,24},{7,9},{15,17},{23,25}} | collective-permute-start | bytes 3145736 | tf_op jit(solution)/shard_map/ppermute | solution.py:219
  5.1 67.7 %collective-permute-start.8 = (bf16[256,2048]{1,0:T(8,128)(2,1)}, bf16[256,2048]{1,0:T(8,128)(2,1)}, u32[]{:S(2)}, u32[]{:S(2)}) collective-permute-start(bf16[256,2048]{1,0:T(8,128)(2,1)} %bitcast.17), channel_id=1, source_target_pairs={{2,0},{4,2},{6,4},{8,6},{10,8},{12,10},{14,12},{16,14},{18,16},{20... | collective-permute-start | bytes 3145736 | tf_op jit(solution)/shard_map/ppermute | solution.py:219
  11.0 66.6 %collective-permute-start.10 = (bf16[256,2048]{1,0:T(8,128)(2,1)}, bf16[256,2048]{1,0:T(8,128)(2,1)S(1)}, u32[]{:S(2)}, u32[]{:S(2)}) collective-permute-start(bf16[256,2048]{1,0:T(8,128)(2,1)} %bitcast.18), channel_id=1, source_target_pairs={{0,30},{2,28},{4,26},{6,24},{8,22},{10,20},{12,18},{14,16},{16,14}... | collective-permute-start | bytes 3145736 | tf_op jit(solution)/shard_map/ppermute | solution.py:219
  70.8 8.8 %copy-start.1 = (bf16[1,4096,512]{2,1,0:T(8,128)(2,1)S(1)}, bf16[1,4096,512]{2,1,0:T(8,128)(2,1)}, u32[]{:S(2)}) copy-start(bf16[1,4096,512]{2,1,0:T(8,128)(2,1)} %param.15) | copy-start | bytes 12582916
  71.0 8.7 %copy-start.4 = (bf16[1,2048]{1,0:T(2,128)(2,1)S(1)}, bf16[1,2048]{1,0:T(2,128)(2,1)}, u32[]{:S(2)}) copy-start(bf16[1,2048]{1,0:T(2,128)(2,1)} %refs_4_.1) | copy-start | bytes 12292
  71.0 8.7 %copy-start.3 = (bf16[1,4096,256]{2,1,0:T(8,128)(2,1)S(1)}, bf16[1,4096,256]{2,1,0:T(8,128)(2,1)}, u32[]{:S(2)}) copy-start(bf16[1,4096,256]{2,1,0:T(8,128)(2,1)} %param.16) | copy-start | bytes 6291460
  71.0 11.6 %collective-permute-start.2 = (bf16[256,2048]{1,0:T(8,128)(2,1)S(1)}, bf16[256,2048]{1,0:T(8,128)(2,1)S(1)}, u32[]{:S(2)}, u32[]{:S(2)}) collective-permute-start(bf16[256,2048]{1,0:T(8,128)(2,1)S(1)} %select_select_fusion.refs_0_), channel_id=1, source_target_pairs={{0,1},{1,0},{2,3},{3,2},{4,5},{5,4},{6,7},{7,6},{8,9},{9,8},{10,11... | collective-permute-start | bytes 3145736 | tf_op jit(solution)/shard_map/ppermute | solution.py:22
  74.1 14.3 %collective-permute-start.9 = (bf16[256,2048]{1,0:T(8,128)(2,1)S(1)}, bf16[256,2048]{1,0:T(8,128)(2,1)S(1)}, u32[]{:S(2)}, u32[]{:S(2)}) collective-permute-start(bf16[256,2048]{1,0:T(8,128)(2,1)S(1)} %broadcast_select_fusion.refs_0_), channel_id=1, source_target_pairs={{0,1},{1,0},{2,3},{3,2},{4,5},{5,4},{6,7},{7,6},{8,9},{9,8},{10,11... | collective-permute-start | bytes 3145736 | tf_op jit(solution)/shard_map/ppermute | solution.py:22
  77.6 10.9 %collective-permute-start.11 = (bf16[256,2048]{1,0:T(8,128)(2,1)S(1)}, bf16[256,2048]{1,0:T(8,128)(2,1)S(1)}, u32[]{:S(2)}, u32[]{:S(2)}) collective-permute-start(bf16[256,2048]{1,0:T(8,128)(2,1)S(1)} %collective-permute-done.10.refs_2_), channel_id=1, source_target_pairs={{0,1},{1,0},{2,3},{3,2},{4,5},{5,4},{6,7},{7,6},{8,9},{9,8},{10,11... | collective-permute-start | bytes 3145736 | tf_op jit(solution)/shard_map/ppermute | solution.py:22
  79.6 2.9 %collective-permute-start.3 = (bf16[1,2048]{1,0:T(2,128)(2,1)S(1)}, bf16[1,2048]{1,0:T(2,128)(2,1)S(1)}, u32[]{:S(2)}, u32[]{:S(2)}) collective-permute-start(bf16[1,2048]{1,0:T(2,128)(2,1)S(1)} %copy-done.4), channel_id=1, source_target_pairs={{0,1},{1,0},{2,3},{3,2},{4,5},{5,4},{6,7},{7,6},{8,9},{9,8},{10,11... | collective-permute-start | bytes 12296 | tf_op jit(solution)/shard_map/ppermute | solution.py:22
  79.7 2.2 %copy-start.2 = (bf16[1,512,4096]{2,1,0:T(8,128)(2,1)S(1)}, bf16[1,512,4096]{2,1,0:T(8,128)(2,1)}, u32[]{:S(2)}) copy-start(bf16[1,512,4096]{2,1,0:T(8,128)(2,1)} %param.17) | copy-start | bytes 12582916
  87.9 10.5 %copy-start.5 = (bf16[1,256,2048]{2,1,0:T(8,128)(2,1)S(1)}, bf16[1,256,2048]{2,1,0:T(8,128)(2,1)}, u32[]{:S(2)}) copy-start(bf16[1,256,2048]{2,1,0:T(8,128)(2,1)} %param.10) | copy-start | bytes 3145732
  87.9 15.1 %collective-permute-start.4 = (bf16[256,2048]{1,0:T(8,128)(2,1)S(1)}, bf16[256,2048]{1,0:T(8,128)(2,1)S(1)}, u32[]{:S(2)}, u32[]{:S(2)}) collective-permute-start(bf16[256,2048]{1,0:T(8,128)(2,1)S(1)} %get-tuple-element.17), channel_id=1, source_target_pairs={{0,1},{1,0},{2,3},{3,2},{4,5},{5,4},{6,7},{7,6},{8,9},{9,8},{10,11... | collective-permute-start | bytes 3145736 | tf_op jit(solution)/shard_map/ppermute | solution.py:22
  97.8 6.7 %collective-permute-start.12 = (bf16[256,2048]{1,0:T(8,128)(2,1)S(1)}, bf16[256,2048]{1,0:T(8,128)(2,1)S(1)}, u32[]{:S(2)}, u32[]{:S(2)}) collective-permute-start(bf16[256,2048]{1,0:T(8,128)(2,1)S(1)} %get-tuple-element.20), channel_id=1, source_target_pairs={{0,1},{1,0},{2,3},{3,2},{4,5},{5,4},{6,7},{7,6},{8,9},{9,8},{10,11... | collective-permute-start | bytes 3145736 | tf_op jit(solution)/shard_map/ppermute | solution.py:22
  97.9 4.3 %collective-permute-start.13 = (f32[256,128]{1,0:T(8,128)S(1)}, f32[256,128]{1,0:T(8,128)S(1)}, u32[]{:S(2)}, u32[]{:S(2)}) collective-permute-start(f32[256,128]{1,0:T(8,128)S(1)} %get-tuple-element.21), channel_id=1, source_target_pairs={{0,1},{1,0},{2,3},{3,2},{4,5},{5,4},{6,7},{7,6},{8,9},{9,8},{10,11... | collective-permute-start | bytes 393224 | tf_op jit(solution)/shard_map/ppermute | solution.py:22
  98.3 49.8 %collective-permute-start.6 = (bf16[256,2048]{1,0:T(8,128)(2,1)S(1)}, bf16[256,2048]{1,0:T(8,128)(2,1)S(1)}, u32[]{:S(2)}, u32[]{:S(2)}) collective-permute-start(bf16[256,2048]{1,0:T(8,128)(2,1)S(1)} %bitcast.21), channel_id=1, source_target_pairs={{8,20},{10,18},{12,16},{14,14},{16,12},{18,10},{20,8},{22,6},{9,21... | collective-permute-start | bytes 3145736 | tf_op jit(solution)/shard_map/ppermute | solution.py:219
  101.2 46.9 %collective-permute-start.7 = (bf16[256,2048]{1,0:T(8,128)(2,1)S(1)}, bf16[256,2048]{1,0:T(8,128)(2,1)S(1)}, u32[]{:S(2)}, u32[]{:S(2)}) collective-permute-start(bf16[256,2048]{1,0:T(8,128)(2,1)S(1)} %bitcast.22), channel_id=1, source_target_pairs={{0,28},{2,26},{4,24},{6,22},{1,29},{3,27},{5,25},{7,23}} | collective-permute-start | bytes 3145736 | tf_op jit(solution)/shard_map/ppermute | solution.py:219
  102.2 46.0 %collective-permute-start.5 = (bf16[256,2048]{1,0:T(8,128)(2,1)S(1)}, bf16[256,2048]{1,0:T(8,128)(2,1)S(1)}, u32[]{:S(2)}, u32[]{:S(2)}) collective-permute-start(bf16[256,2048]{1,0:T(8,128)(2,1)S(1)} %collective-permute-done.1), channel_id=1, source_target_pairs={{26,4},{28,2},{30,0},{27,5},{29,3},{31,1}} | collective-permute-start | bytes 3145736 | tf_op jit(solution)/shard_map/ppermute | solution.py:219
  104.5 43.7 %copy-start = (bf16[256,2048]{1,0:T(8,128)(2,1)S(1)}, bf16[256,2048]{1,0:T(8,128)(2,1)}, u32[]{:S(2)}) copy-start(bf16[256,2048]{1,0:T(8,128)(2,1)} %last) | copy-start | bytes 3145732
where the time goes:
time: 149 us
  waiting for transfers between devices  104 us (70%)
  starting transfers between devices  21.1 us (14%)
  Pallas kernels  16.3 us (11%)
  other arithmetic  5.11 us (3%)
  local copies, waits for them, and re-layouts  2.21 us (1%)
    ppermute x7, waiting for transfers between devices, send(): return lax.ppermute(value, 'section', pairs)  104 us
    pallas_call x4, Pallas kernels, call(): pl.pallas_call(functools.partial(kernel, count, heads), out_shape=out_sha...  16.3 us
    ppermute x7, starting transfers between devices, send(): return lax.ppermute(value, 'section', pairs)  14.7 us
    ppermute x7, starting transfers between devices, rotate(): lax.ppermute(value, axis, [(i, (i - k) % count) for i in range(count)])  6.39 us
  transfers between devices with their start and end apart: 14, of which 4 were waited for; matrix products, arithmetic and copies ran while one was open for 3% of the time, Pallas kernels for 10%

commit v1 on v0

--- a/solution.py
+++ b/solution.py
@@ -174,12 +174,28 @@
         copy.wait()
 
 
-def merge_kernel(count, block, relayed, near, far, last, out, sem):
+def choose_kernel(count, tests, *refs):
+    *sources, out, sem = refs
     place, sections = lax.axis_index("section"), lax.axis_size("section")
-    ends = (0, block - 1, sections - block - 1, sections - 1, sections)
-    for low, high, source in zip(ends, ends[1:], (relayed, near, far, last)):
-
-        @pl.when((place >= low) & (place < high))
+    for test, source in zip(tests(place, sections), sources):
+
+        @pl.when(test)
+        def _():
+            copy = pltpu.make_async_copy(source, out, sem)
+            copy.start()
+            copy.wait()
+
+
+def merge_kernel(count, block, relayed, alone, direct, last, out, sem):
+    place, sections = lax.axis_index("section"), lax.axis_size("section")
+    is_last = place == sections - 1
+    is_alone = place == sections - 1 - block
+    is_relayed = place < block - 1
+    is_direct = jnp.logical_not(is_last | is_alone | is_relayed)
+    chosen = ((is_relayed, relayed), (is_alone, alone), (is_direct, direct), (is_last, last))
+    for here, source in chosen:
+
+        @pl.when(here)
         def _():
             copy = pltpu.make_async_copy(source, out, sem)
             copy.start()
@@ -203,7 +219,6 @@
 ):
     sections = lax.axis_size("section")
     count = lax.axis_size("tensor")
-    position = lax.axis_index("section")
     held, grads_held, stash_held = outbox[0], grad_outbox[0], stash_held[0]
     seq, width = held.shape
     model = width * count
@@ -218,14 +233,17 @@
     def send(value, pairs):
         return lax.ppermute(value, "section", pairs)
 
+    def early(t):
+        return (t % block == 0) | (t > high)
+
     up = [(s, s + 1) for s in range(sections - 1)]
-    crossing = send(held, [(s, t) for s, t in up if t % block == 0])
+    soon = send(held, [(s, t) for s, t in up if early(t)])
+    coming = send(grads_held, [(t, s) for s, t in up])
     fetched = send(stash_held, [(s, sections - 1 - s) for s in range(sections)])
-    coming = send(grads_held, [(t, s) for s, t in up])
-    inside = send(held, [(s, t) for s, t in up if t % block])
-    evicted_near = send(held, [(s, sections - 2 - s) for s in range(block, high)])
-    evicted_far = send(held, [(s, sections - 2 - s) for s in range(block)])
-    relayed = send(inside, [(s, sections - 1 - s) for s in range(high + 1, sections)])
+    later = send(held, [(s, t) for s, t in up if not early(t)])
+    evicted = send(held, [(s, sections - 2 - s) for s in range(high) if s != block - 1])
+    alone = send(held, [(block - 1, sections - 1 - block)])
+    relayed = send(soon, [(s, sections - 1 - s) for s in range(high + 1, sections)])
     gains = gathered(norm_gain, "tensor")
 
     normed = pltpu.VMEM((seq, model), BF16)
@@ -239,8 +257,19 @@
         [pltpu.SemaphoreType.DMA((3,))], 0, 2 * moved, far_in=1,
     )
     bs = gathered(fetched, "tensor")
-    arrived = jnp.where(position % block == 0, crossing, inside)
-    x_shard = jnp.where(position == 0, embedded, arrived)
+
+    def x_tests(place, sections):
+        is_early = (place % block == 0) | (place > high)
+        return place == 0, is_early & (place != 0), jnp.logical_not(is_early)
+
+    def choose(tests, ins):
+        (out,) = call(
+            choose_kernel, count, tests, ins, [shape((seq, width), BF16)],
+            [pltpu.SemaphoreType.DMA], 0, 4 * seq * width,
+        )
+        return out
+
+    x_shard = choose(x_tests, [embedded, soon, later])
     xs = gathered(x_shard, "tensor")
     parts = call(
         forward_kernel, count, heads,
@@ -248,10 +277,7 @@
         [normed, pltpu.VMEM((seq, qcols), BF16)],
         proj + out_flops, moved,
     )
-    mixed = reduced(parts, "tensor")
-    section_out = (x_shard.astype(F32) + mixed).astype(BF16)
-
-    g_shard = jnp.where(position == sections - 1, loss_grad, coming)
+    g_shard = choose(lambda place, n: (place == n - 1, place != n - 1), [loss_grad, coming])
     gs = gathered(g_shard, "tensor")
     *terms, total, inv = call(
         backward_kernel, count, heads,
@@ -272,10 +298,14 @@
     result = (
         g_shard.astype(F32) + inv * scaled - fetched.astype(F32) * inv**3 * (total / model)
     ).astype(BF16)
+    own, *others = parts
+    own, _ = lax.optimization_barrier((own, result))
+    mixed = reduced([own, *others], "tensor")
+    section_out = (x_shard.astype(F32) + mixed).astype(BF16)
     last, _ = lax.optimization_barrier((embedded, (result, section_out)))
     (evicted,) = call(
         merge_kernel, count, block,
-        [relayed, evicted_near, evicted_far, last], [shape((seq, width), BF16)],
+        [relayed, alone, evicted, last], [shape((seq, width), BF16)],
         [pltpu.SemaphoreType.DMA], 0, 4 * seq * width, far_out=1,
     )
     return section_out[None], evicted[None], result[None]

time: 149 us -> 148 us (level)
  the two profiles are of different devices: /device:TPU:17 before, /device:TPU:6 now
where the time goes in v1:
time: 148 us
  waiting for transfers between devices  105 us (71%)
  starting transfers between devices  18.3 us (12%)
  Pallas kernels  16.5 us (11%)
  other arithmetic  3.64 us (2%)
  local copies, waits for them, and re-layouts  3.43 us (2%)
    ppermute x7, waiting for transfers between devices, send(): return lax.ppermute(value, 'section', pairs)  105 us
    ppermute x7, starting transfers between devices, send(): return lax.ppermute(value, 'section', pairs)  17 us
    pallas_call x6, Pallas kernels, call(): pl.pallas_call(functools.partial(kernel, count, heads), out_shape=out_sha...  16.5 us
    unnamed x14, local copies, waits for them, and re-layouts  3.43 us
  transfers between devices with their start and end apart: 14, of which 5 were waited for; matrix products, arithmetic and copies ran while one was open for 2% of the time, Pallas kernels for 11%

profile of v1, /device:TPU:6, one launch (start us, length us, event | category | flops | bytes accessed | tf_op | source)
XLA Modules:
  0.0 147.7 jit_solution(7709592770043643868)
XLA Ops:
  0.6 2.6 %collective-permute-start.4 = (bf16[256,2048]{1,0:T(8,128)(2,1)}, bf16[256,2048]{1,0:T(8,128)(2,1)S(1)}, u32[]{:S(2)}, u32[]{:S(2)}) collective-permute-start(bf16[256,2048]{1,0:T(8,128)(2,1)} %bitcast.17), channel_id=1, source_target_pairs={{2,0},{4,2},{6,4},{8,6},{10,8},{12,10},{14,12},{16,14},{18,16},{20... | collective-permute-start | bytes 3145736 | tf_op jit(solution)/shard_map/ppermute | solution.py:234
  3.2 5.4 %collective-permute-start.6 = (bf16[256,2048]{1,0:T(8,128)(2,1)}, bf16[256,2048]{1,0:T(8,128)(2,1)S(1)}, u32[]{:S(2)}, u32[]{:S(2)}) collective-permute-start(bf16[256,2048]{1,0:T(8,128)(2,1)} %bitcast.18), channel_id=1, source_target_pairs={{0,30},{2,28},{4,26},{6,24},{8,22},{10,20},{12,18},{14,16},{16,14}... | collective-permute-start | bytes 3145736 | tf_op jit(solution)/shard_map/ppermute | solution.py:234
  8.6 1.6 %collective-permute-start = (bf16[256,2048]{1,0:T(8,128)(2,1)}, bf16[256,2048]{1,0:T(8,128)(2,1)S(1)}, u32[]{:S(2)}, u32[]{:S(2)}) collective-permute-start(bf16[256,2048]{1,0:T(8,128)(2,1)} %bitcast.19), channel_id=1, source_target_pairs={{6,8},{14,16},{22,24},{24,26},{26,28},{28,30},{7,9},{15,17},{23,25... | collective-permute-start | bytes 3145736 | tf_op jit(solution)/shard_map/ppermute | solution.py:234
  10.2 1.3 collective-permute-start.1
  11.5 36.9 %collective-permute-done.4.refs_1_ = bf16[256,2048]{1,0:T(8,128)(2,1)S(1)} collective-permute-done((bf16[256,2048]{1,0:T(8,128)(2,1)}, bf16[256,2048]{1,0:T(8,128)(2,1)S(1)}, u32[]{:S(2)}, u32[]{:S(2)}) %collective-permute-start.4) | collective-permute-done | bytes 1048608 | tf_op jit(solution)/shard_map/ppermute | solution.py:234
  48.4 1.2 copy-done.4
  49.8 6.0 %collective-permute-done.6.refs_2_ = bf16[256,2048]{1,0:T(8,128)(2,1)S(1)} collective-permute-done((bf16[256,2048]{1,0:T(8,128)(2,1)}, bf16[256,2048]{1,0:T(8,128)(2,1)S(1)}, u32[]{:S(2)}, u32[]{:S(2)}) %collective-permute-start.6) | collective-permute-done | bytes 1048608 | tf_op jit(solution)/shard_map/ppermute | solution.py:234
  55.8 17.3 %collective-permute-done.refs_1_ = bf16[256,2048]{1,0:T(8,128)(2,1)S(1)} collective-permute-done((bf16[256,2048]{1,0:T(8,128)(2,1)}, bf16[256,2048]{1,0:T(8,128)(2,1)S(1)}, u32[]{:S(2)}, u32[]{:S(2)}) %collective-permute-start) | collective-permute-done | bytes 1048608 | tf_op jit(solution)/shard_map/ppermute | solution.py:234
  73.3 0.5 collective-permute-start.3
  73.8 2.2 %copy-done.1 = bf16[1,512,4096]{2,1,0:T(8,128)(2,1)S(1)} copy-done((bf16[1,512,4096]{2,1,0:T(8,128)(2,1)S(1)}, bf16[1,512,4096]{2,1,0:T(8,128)(2,1)}, u32[]{:S(2)}) %copy-start.1) | copy-done | bytes 4194328
  76.0 0.7 shard_map.113
  76.8 9.4 %shard_map.116 = (bf16[256,2048]{1,0:T(8,128)(2,1)S(1)}, bf16[256,2048]{1,0:T(8,128)(2,1)S(1)}, f32[256,128]{1,0:T(8,128)S(1)}, f32[256,128]{1,0:T(8,128)S(1)}) custom-call(bf16[256,2048]{1,0:T(8,128)(2,1)S(1)} %shard_map.115.refs_0_, bf16[256,2048]{1,0:T(8,128)(2,1)S(1)} %collective-permute-done.5.refs_1_, ...), custom_call_target="tpu_custom_call" | custom-call | flops 4294967296 | bytes 10485760 | tf_op jit(solution)/shard_map/pallas_call | solution.py:206
  86.2 0.2 collective-permute-start.8
  86.3 5.2 %shard_map.114 = (bf16[256,2048]{1,0:T(8,128)(2,1)S(1)}, bf16[256,2048]{1,0:T(8,128)(2,1)S(1)}) custom-call(bf16[256,2048]{1,0:T(8,128)(2,1)S(1)} %shard_map.112.refs_0_, bf16[256,2048]{1,0:T(8,128)(2,1)S(1)} %collective-permute-done.2.refs_1_, bf16[1,2048]{1,0:T(2,128)(2,1)S(1)} %copy-done.5, bf16[1,2048]{1,0:T(2,128)(2,1)S(1)} %collective-permute-done.3.refs_3_.refs_5_, ...), custom_call_target="tpu_custom_call" | custom-call | flops 2684354560 | bytes 10485760 | tf_op jit(solution)/shard_map/pallas_call | solution.py:206
  91.6 0.5 collective-permute-start.10
  92.2 4.1 %collective-permute-start.12 = (bf16[256,2048]{1,0:T(8,128)(2,1)S(1)}, bf16[256,2048]{1,0:T(8,128)(2,1)S(1)}, u32[]{:S(2)}, u32[]{:S(2)}) collective-permute-start(bf16[256,2048]{1,0:T(8,128)(2,1)S(1)} %bitcast.21), channel_id=1, source_target_pairs={{6,22},{7,23}} | collective-permute-start | bytes 3145736 | tf_op jit(solution)/shard_map/ppermute | solution.py:234
  96.3 1.3 collective-permute-start.13
  97.6 0.1 slice_reduce_fusion
  97.7 0.7 collective-permute-start.11
  98.6 1.8 %subtract_convert_fusion = bf16[256,2048]{1,0:T(8,128)(2,1)} fusion(bf16[256,2048]{1,0:T(8,128)(2,1)S(1)} %collective-permute-done.6.refs_2_, bf16[256,2048]{1,0:T(8,128)(2,1)S(1)} %collective-permute-done.8, bf16[256,2048]{1,0:T(8,128)(2,1)S(1)} %get-tuple-element.19, bf16[256,2048]{1,0:T(8,128)(2,1)S(1)} %shard_map.115.refs_0_, f32[256]{0:T(256)S(1)} %fusion.2, ...), kind=kLoop, calls=%fused_computation.1 | loop fusion | flops 6291456 | bytes 5254144 | tf_op jit(solution)/shard_map/convert_element_type | solution.py:300
  100.5 1.5 %add_convert_fusion = bf16[256,2048]{1,0:T(8,128)(2,1)} fusion(bf16[256,2048]{1,0:T(8,128)(2,1)S(1)} %collective-permute-done.10, bf16[256,2048]{1,0:T(8,128)(2,1)S(1)} %get-tuple-element.22, bf16[256,2048]{1,0:T(8,128)(2,1)S(1)} %shard_map.112.refs_0_), kind=kLoop, calls=%fused_computation | loop fusion | flops 3145728 | bytes 4194304 | tf_op jit(solution)/shard_map/convert_element_type | solution.py:304
  102.0 17.2 %collective-permute-done.12.alone = bf16[256,2048]{1,0:T(8,128)(2,1)S(1)} collective-permute-done((bf16[256,2048]{1,0:T(8,128)(2,1)S(1)}, bf16[256,2048]{1,0:T(8,128)(2,1)S(1)}, u32[]{:S(2)}, u32[]{:S(2)}) %collective-permute-start.12) | collective-permute-done | bytes 1048608 | tf_op jit(solution)/shard_map/ppermute | solution.py:234
  119.2 27.5 %collective-permute-done.13.direct = bf16[256,2048]{1,0:T(8,128)(2,1)S(1)} collective-permute-done((bf16[256,2048]{1,0:T(8,128)(2,1)S(1)}, bf16[256,2048]{1,0:T(8,128)(2,1)S(1)}, u32[]{:S(2)}, u32[]{:S(2)}) %collective-permute-start.13) | collective-permute-done | bytes 1048608 | tf_op jit(solution)/shard_map/ppermute | solution.py:234
  146.7 1.0 shard_map.117
  (29 shorter events, 0.6 us)
Async XLA Ops:
  0.6 72.5 %copy-start.2 = (bf16[256,2048]{1,0:T(8,128)(2,1)S(1)}, bf16[256,2048]{1,0:T(8,128)(2,1)}, u32[]{:S(2)}) copy-start(bf16[256,2048]{1,0:T(8,128)(2,1)} %last) | copy-start | bytes 3145732
  0.6 47.8 %collective-permute-start.4 = (bf16[256,2048]{1,0:T(8,128)(2,1)}, bf16[256,2048]{1,0:T(8,128)(2,1)S(1)}, u32[]{:S(2)}, u32[]{:S(2)}) collective-permute-start(bf16[256,2048]{1,0:T(8,128)(2,1)} %bitcast.17), channel_id=1, source_target_pairs={{2,0},{4,2},{6,4},{8,6},{10,8},{12,10},{14,12},{16,14},{18,16},{20... | collective-permute-start | bytes 3145736 | tf_op jit(solution)/shard_map/ppermute | solution.py:234
  3.2 52.6 %collective-permute-start.6 = (bf16[256,2048]{1,0:T(8,128)(2,1)}, bf16[256,2048]{1,0:T(8,128)(2,1)S(1)}, u32[]{:S(2)}, u32[]{:S(2)}) collective-permute-start(bf16[256,2048]{1,0:T(8,128)(2,1)} %bitcast.18), channel_id=1, source_target_pairs={{0,30},{2,28},{4,26},{6,24},{8,22},{10,20},{12,18},{14,16},{16,14}... | collective-permute-start | bytes 3145736 | tf_op jit(solution)/shard_map/ppermute | solution.py:234
  8.6 64.5 %collective-permute-start = (bf16[256,2048]{1,0:T(8,128)(2,1)}, bf16[256,2048]{1,0:T(8,128)(2,1)S(1)}, u32[]{:S(2)}, u32[]{:S(2)}) collective-permute-start(bf16[256,2048]{1,0:T(8,128)(2,1)} %bitcast.19), channel_id=1, source_target_pairs={{6,8},{14,16},{22,24},{24,26},{26,28},{28,30},{7,9},{15,17},{23,25... | collective-permute-start | bytes 3145736 | tf_op jit(solution)/shard_map/ppermute | solution.py:234
  10.2 62.9 %collective-permute-start.1 = (bf16[256,2048]{1,0:T(8,128)(2,1)}, bf16[256,2048]{1,0:T(8,128)(2,1)S(1)}, u32[]{:S(2)}, u32[]{:S(2)}) collective-permute-start(bf16[256,2048]{1,0:T(8,128)(2,1)} %bitcast.20), channel_id=1, source_target_pairs={{0,2},{2,4},{4,6},{8,10},{10,12},{12,14},{16,18},{18,20},{20,22},{... | collective-permute-start | bytes 3145736 | tf_op jit(solution)/shard_map/ppermute | solution.py:234
  48.4 1.2 copy-start.4
  49.6 23.7 %copy-start.5 = (bf16[1,2048]{1,0:T(2,128)(2,1)S(1)}, bf16[1,2048]{1,0:T(2,128)(2,1)}, u32[]{:S(2)}) copy-start(bf16[1,2048]{1,0:T(2,128)(2,1)} %refs_4_.1) | copy-start | bytes 12292
  49.6 24.2 %copy-start.3 = (bf16[1,4096,256]{2,1,0:T(8,128)(2,1)S(1)}, bf16[1,4096,256]{2,1,0:T(8,128)(2,1)}, u32[]{:S(2)}) copy-start(bf16[1,4096,256]{2,1,0:T(8,128)(2,1)} %param.16) | copy-start | bytes 6291460
  49.7 24.1 %copy-start = (bf16[1,4096,512]{2,1,0:T(8,128)(2,1)S(1)}, bf16[1,4096,512]{2,1,0:T(8,128)(2,1)}, u32[]{:S(2)}) copy-start(bf16[1,4096,512]{2,1,0:T(8,128)(2,1)} %param.15) | copy-start | bytes 12582916
  49.7 27.0 %collective-permute-start.5 = (bf16[256,2048]{1,0:T(8,128)(2,1)S(1)}, bf16[256,2048]{1,0:T(8,128)(2,1)S(1)}, u32[]{:S(2)}, u32[]{:S(2)}) collective-permute-start(bf16[256,2048]{1,0:T(8,128)(2,1)S(1)} %shard_map.115.refs_0_), channel_id=1, source_target_pairs={{0,1},{1,0},{2,3},{3,2},{4,5},{5,4},{6,7},{7,6},{8,9},{9,8},{10,11... | collective-permute-start | bytes 3145736 | tf_op jit(solution)/shard_map/ppermute | solution.py:22
  55.8 20.9 %collective-permute-start.7 = (bf16[256,2048]{1,0:T(8,128)(2,1)S(1)}, bf16[256,2048]{1,0:T(8,128)(2,1)S(1)}, u32[]{:S(2)}, u32[]{:S(2)}) collective-permute-start(bf16[256,2048]{1,0:T(8,128)(2,1)S(1)} %collective-permute-done.6.refs_2_), channel_id=1, source_target_pairs={{0,1},{1,0},{2,3},{3,2},{4,5},{5,4},{6,7},{7,6},{8,9},{9,8},{10,11... | collective-permute-start | bytes 3145736 | tf_op jit(solution)/shard_map/ppermute | solution.py:22
  73.2 13.1 %collective-permute-start.2 = (bf16[256,2048]{1,0:T(8,128)(2,1)S(1)}, bf16[256,2048]{1,0:T(8,128)(2,1)S(1)}, u32[]{:S(2)}, u32[]{:S(2)}) collective-permute-start(bf16[256,2048]{1,0:T(8,128)(2,1)S(1)} %shard_map.112.refs_0_), channel_id=1, source_target_pairs={{0,1},{1,0},{2,3},{3,2},{4,5},{5,4},{6,7},{7,6},{8,9},{9,8},{10,11... | collective-permute-start | bytes 3145736 | tf_op jit(solution)/shard_map/ppermute | solution.py:22
  73.3 3.4 %collective-permute-start.3 = (bf16[1,2048]{1,0:T(2,128)(2,1)S(1)}, bf16[1,2048]{1,0:T(2,128)(2,1)S(1)}, u32[]{:S(2)}, u32[]{:S(2)}) collective-permute-start(bf16[1,2048]{1,0:T(2,128)(2,1)S(1)} %copy-done.5), channel_id=1, source_target_pairs={{0,1},{1,0},{2,3},{3,2},{4,5},{5,4},{6,7},{7,6},{8,9},{9,8},{10,11... | collective-permute-start | bytes 12296 | tf_op jit(solution)/shard_map/ppermute | solution.py:22
  73.8 2.2 %copy-start.1 = (bf16[1,512,4096]{2,1,0:T(8,128)(2,1)S(1)}, bf16[1,512,4096]{2,1,0:T(8,128)(2,1)}, u32[]{:S(2)}) copy-start(bf16[1,512,4096]{2,1,0:T(8,128)(2,1)} %param.17) | copy-start | bytes 12582916
  86.2 6.0 %copy-start.6 = (bf16[1,256,2048]{2,1,0:T(8,128)(2,1)S(1)}, bf16[1,256,2048]{2,1,0:T(8,128)(2,1)}, u32[]{:S(2)}) copy-start(bf16[1,256,2048]{2,1,0:T(8,128)(2,1)} %param.10) | copy-start | bytes 3145732
  86.2 12.4 %collective-permute-start.8 = (bf16[256,2048]{1,0:T(8,128)(2,1)S(1)}, bf16[256,2048]{1,0:T(8,128)(2,1)S(1)}, u32[]{:S(2)}, u32[]{:S(2)}) collective-permute-start(bf16[256,2048]{1,0:T(8,128)(2,1)S(1)} %get-tuple-element.20), channel_id=1, source_target_pairs={{0,1},{1,0},{2,3},{3,2},{4,5},{5,4},{6,7},{7,6},{8,9},{9,8},{10,11... | collective-permute-start | bytes 3145736 | tf_op jit(solution)/shard_map/ppermute | solution.py:22
  91.6 8.9 %collective-permute-start.10 = (bf16[256,2048]{1,0:T(8,128)(2,1)S(1)}, bf16[256,2048]{1,0:T(8,128)(2,1)S(1)}, u32[]{:S(2)}, u32[]{:S(2)}) collective-permute-start(bf16[256,2048]{1,0:T(8,128)(2,1)S(1)} %get-tuple-element.23), channel_id=1, source_target_pairs={{0,1},{1,0},{2,3},{3,2},{4,5},{5,4},{6,7},{7,6},{8,9},{9,8},{10,11... | collective-permute-start | bytes 3145736 | tf_op jit(solution)/shard_map/ppermute | solution.py:22
  92.1 5.7 %collective-permute-start.9 = (f32[256,128]{1,0:T(8,128)S(1)}, f32[256,128]{1,0:T(8,128)S(1)}, u32[]{:S(2)}, u32[]{:S(2)}) collective-permute-start(f32[256,128]{1,0:T(8,128)S(1)} %get-tuple-element.21), channel_id=1, source_target_pairs={{0,1},{1,0},{2,3},{3,2},{4,5},{5,4},{6,7},{7,6},{8,9},{9,8},{10,11... | collective-permute-start | bytes 393224 | tf_op jit(solution)/shard_map/ppermute | solution.py:22
  92.2 27.0 %collective-permute-start.12 = (bf16[256,2048]{1,0:T(8,128)(2,1)S(1)}, bf16[256,2048]{1,0:T(8,128)(2,1)S(1)}, u32[]{:S(2)}, u32[]{:S(2)}) collective-permute-start(bf16[256,2048]{1,0:T(8,128)(2,1)S(1)} %bitcast.21), channel_id=1, source_target_pairs={{6,22},{7,23}} | collective-permute-start | bytes 3145736 | tf_op jit(solution)/shard_map/ppermute | solution.py:234
  96.3 50.5 %collective-permute-start.13 = (bf16[256,2048]{1,0:T(8,128)(2,1)S(1)}, bf16[256,2048]{1,0:T(8,128)(2,1)S(1)}, u32[]{:S(2)}, u32[]{:S(2)}) collective-permute-start(bf16[256,2048]{1,0:T(8,128)(2,1)S(1)} %bitcast.22), channel_id=1, source_target_pairs={{0,28},{2,26},{4,24},{8,20},{10,18},{12,16},{14,14},{16,12},{18,10... | collective-permute-start | bytes 3145736 | tf_op jit(solution)/shard_map/ppermute | solution.py:234
  97.7 49.0 %collective-permute-start.11 = (bf16[256,2048]{1,0:T(8,128)(2,1)S(1)}, bf16[256,2048]{1,0:T(8,128)(2,1)S(1)}, u32[]{:S(2)}, u32[]{:S(2)}) collective-permute-start(bf16[256,2048]{1,0:T(8,128)(2,1)S(1)} %collective-permute-done.refs_1_), channel_id=1, source_target_pairs={{26,4},{28,2},{30,0},{27,5},{29,3},{31,1}} | collective-permute-start | bytes 3145736 | tf_op jit(solution)/shard_map/ppermute | solution.py:234

commit v2 on v1

--- a/solution.py
+++ b/solution.py
@@ -291,17 +291,17 @@
         ],
         2 * proj + out_flops, moved,
     )
-    d_normed = reduced(terms, "tensor")
+    mixed = reduced(parts, "tensor")
+    section_out = (x_shard.astype(F32) + mixed).astype(BF16)
+    own, *others = terms
+    own, _ = lax.optimization_barrier((own, section_out))
+    d_normed = reduced([own, *others], "tensor")
     total = sum(gathered(total, "tensor"))[:, :1]
     inv = inv[:, :1]
     scaled = d_normed * norm_gain.astype(F32)
     result = (
         g_shard.astype(F32) + inv * scaled - fetched.astype(F32) * inv**3 * (total / model)
     ).astype(BF16)
-    own, *others = parts
-    own, _ = lax.optimization_barrier((own, result))
-    mixed = reduced([own, *others], "tensor")
-    section_out = (x_shard.astype(F32) + mixed).astype(BF16)
     last, _ = lax.optimization_barrier((embedded, (result, section_out)))
     (evicted,) = call(
         merge_kernel, count, block,

time: 148 us -> 149 us (level)
  the two profiles are of different devices: /device:TPU:6 before, /device:TPU:10 now
where the time goes in v2:
time: 149 us
  waiting for transfers between devices  106 us (71%)
  starting transfers between devices  17.8 us (12%)
  Pallas kernels  16.4 us (11%)
  local copies, waits for them, and re-layouts  4.69 us (3%)
  other arithmetic  3.63 us (2%)
    ppermute x7, waiting for transfers between devices, send(): return lax.ppermute(value, 'section', pairs)  105 us
    pallas_call x6, Pallas kernels, call(): pl.pallas_call(functools.partial(kernel, count, heads), out_shape=out_sha...  16.4 us
    ppermute x7, starting transfers between devices, send(): return lax.ppermute(value, 'section', pairs)  16.3 us
    unnamed x16, local copies, waits for them, and re-layouts  4.69 us
  transfers between devices with their start and end apart: 14, of which 4 were waited for; matrix products, arithmetic and copies ran while one was open for 2% of the time, Pallas kernels for 10%

profile of v2, /device:TPU:10, one launch (start us, length us, event | category | flops | bytes accessed | tf_op | source)
XLA Modules:
  0.0 149.1 jit_solution(1809053984132329379)
XLA Ops:
  0.6 0.7 collective-permute-start
  1.4 3.4 %collective-permute-start.1 = (bf16[256,2048]{1,0:T(8,128)(2,1)}, bf16[256,2048]{1,0:T(8,128)(2,1)S(1)}, u32[]{:S(2)}, u32[]{:S(2)}) collective-permute-start(bf16[256,2048]{1,0:T(8,128)(2,1)} %bitcast.20), channel_id=1, source_target_pairs={{0,2},{2,4},{4,6},{8,10},{10,12},{12,14},{16,18},{18,20},{20,22},{... | collective-permute-start | bytes 3145736 | tf_op jit(solution)/shard_map/ppermute | solution.py:234
  4.8 2.5 %collective-permute-start.8 = (bf16[256,2048]{1,0:T(8,128)(2,1)}, bf16[256,2048]{1,0:T(8,128)(2,1)S(1)}, u32[]{:S(2)}, u32[]{:S(2)}) collective-permute-start(bf16[256,2048]{1,0:T(8,128)(2,1)} %bitcast.17), channel_id=1, source_target_pairs={{2,0},{4,2},{6,4},{8,6},{10,8},{12,10},{14,12},{16,14},{18,16},{20... | collective-permute-start | bytes 3145736 | tf_op jit(solution)/shard_map/ppermute | solution.py:234
  7.3 4.7 %collective-permute-start.10 = (bf16[256,2048]{1,0:T(8,128)(2,1)}, bf16[256,2048]{1,0:T(8,128)(2,1)S(1)}, u32[]{:S(2)}, u32[]{:S(2)}) collective-permute-start(bf16[256,2048]{1,0:T(8,128)(2,1)} %bitcast.18), channel_id=1, source_target_pairs={{0,30},{2,28},{4,26},{6,24},{8,22},{10,20},{12,18},{14,16},{16,14}... | collective-permute-start | bytes 3145736 | tf_op jit(solution)/shard_map/ppermute | solution.py:234
  12.0 40.0 %collective-permute-done.1.refs_2_ = bf16[256,2048]{1,0:T(8,128)(2,1)S(1)} collective-permute-done((bf16[256,2048]{1,0:T(8,128)(2,1)}, bf16[256,2048]{1,0:T(8,128)(2,1)S(1)}, u32[]{:S(2)}, u32[]{:S(2)}) %collective-permute-start.1) | collective-permute-done | bytes 1048608 | tf_op jit(solution)/shard_map/ppermute | solution.py:234
  52.1 1.2 copy-done.2
  53.5 23.3 %collective-permute-done.8.refs_1_ = bf16[256,2048]{1,0:T(8,128)(2,1)S(1)} collective-permute-done((bf16[256,2048]{1,0:T(8,128)(2,1)}, bf16[256,2048]{1,0:T(8,128)(2,1)S(1)}, u32[]{:S(2)}, u32[]{:S(2)}) %collective-permute-start.8) | collective-permute-done | bytes 1048608 | tf_op jit(solution)/shard_map/ppermute | solution.py:234
  76.7 1.2 copy-done.5
  78.1 0.5 collective-permute-start.11
  78.7 2.2 %copy-done.1 = bf16[1,512,4096]{2,1,0:T(8,128)(2,1)S(1)} copy-done((bf16[1,512,4096]{2,1,0:T(8,128)(2,1)S(1)}, bf16[1,512,4096]{2,1,0:T(8,128)(2,1)}, u32[]{:S(2)}) %copy-start.1) | copy-done | bytes 4194328
  80.9 0.7 shard_map.113
  81.6 0.6 collective-permute-done.3.refs_3_.refs_5_
  82.3 5.2 %shard_map.114 = (bf16[256,2048]{1,0:T(8,128)(2,1)S(1)}, bf16[256,2048]{1,0:T(8,128)(2,1)S(1)}) custom-call(bf16[256,2048]{1,0:T(8,128)(2,1)S(1)} %shard_map.112.refs_0_, bf16[256,2048]{1,0:T(8,128)(2,1)S(1)} %collective-permute-done.2.refs_1_, bf16[1,2048]{1,0:T(2,128)(2,1)S(1)} %copy-done.6, bf16[1,2048]{1,0:T(2,128)(2,1)S(1)} %collective-permute-done.3.refs_3_.refs_5_, ...), custom_call_target="tpu_custom_call" | custom-call | flops 2684354560 | bytes 10485760 | tf_op jit(solution)/shard_map/pallas_call | solution.py:206
  87.5 0.2 collective-permute-start.4
  87.8 9.3 %shard_map.116 = (bf16[256,2048]{1,0:T(8,128)(2,1)S(1)}, bf16[256,2048]{1,0:T(8,128)(2,1)S(1)}, f32[256,128]{1,0:T(8,128)S(1)}, f32[256,128]{1,0:T(8,128)S(1)}) custom-call(bf16[256,2048]{1,0:T(8,128)(2,1)S(1)} %shard_map.115.refs_0_, bf16[256,2048]{1,0:T(8,128)(2,1)S(1)} %collective-permute-done.9.refs_1_, ...), custom_call_target="tpu_custom_call" | custom-call | flops 4294967296 | bytes 10485760 | tf_op jit(solution)/shard_map/pallas_call | solution.py:206
  97.1 0.4 collective-permute-start.12
  97.6 0.7 collective-permute-start.6
  98.4 3.5 %collective-permute-start.7 = (bf16[256,2048]{1,0:T(8,128)(2,1)S(1)}, bf16[256,2048]{1,0:T(8,128)(2,1)S(1)}, u32[]{:S(2)}, u32[]{:S(2)}) collective-permute-start(bf16[256,2048]{1,0:T(8,128)(2,1)S(1)} %bitcast.22), channel_id=1, source_target_pairs={{0,28},{2,26},{4,24},{8,20},{10,18},{12,16},{14,14},{16,12},{18,10... | collective-permute-start | bytes 3145736 | tf_op jit(solution)/shard_map/ppermute | solution.py:234
  101.9 0.1 slice_reduce_fusion
  102.0 0.7 collective-permute-start.5
  102.9 1.5 %add_convert_fusion = bf16[256,2048]{1,0:T(8,128)(2,1)} fusion(bf16[256,2048]{1,0:T(8,128)(2,1)S(1)} %collective-permute-done.4, bf16[256,2048]{1,0:T(8,128)(2,1)S(1)} %get-tuple-element.17, bf16[256,2048]{1,0:T(8,128)(2,1)S(1)} %shard_map.112.refs_0_), kind=kLoop, calls=%fused_computation.1 | loop fusion | flops 3145728 | bytes 4194304 | tf_op jit(solution)/shard_map/convert_element_type | solution.py:295
  104.4 1.9 %subtract_convert_fusion = bf16[256,2048]{1,0:T(8,128)(2,1)} fusion(bf16[256,2048]{1,0:T(8,128)(2,1)S(1)} %collective-permute-done.10.refs_2_, bf16[256,2048]{1,0:T(8,128)(2,1)S(1)} %collective-permute-done.12, bf16[256,2048]{1,0:T(8,128)(2,1)S(1)} %get-tuple-element.21, bf16[256,2048]{1,0:T(8,128)(2,1)S(1)} %shard_map.115.refs_0_, f32[256]{0:T(256)S(1)} %fusion.2, ...), kind=kLoop, calls=%fused_computation | loop fusion | flops 6291456 | bytes 5254144 | tf_op jit(solution)/shard_map/convert_element_type | solution.py:304
  106.3 41.9 %collective-permute-done.7.direct = bf16[256,2048]{1,0:T(8,128)(2,1)S(1)} collective-permute-done((bf16[256,2048]{1,0:T(8,128)(2,1)S(1)}, bf16[256,2048]{1,0:T(8,128)(2,1)S(1)}, u32[]{:S(2)}, u32[]{:S(2)}) %collective-permute-start.7) | collective-permute-done | bytes 1048608 | tf_op jit(solution)/shard_map/ppermute | solution.py:234
  148.2 1.0 shard_map.117
  (31 shorter events, 0.7 us)
Async XLA Ops:
  0.6 11.4 %collective-permute-start = (bf16[256,2048]{1,0:T(8,128)(2,1)}, bf16[256,2048]{1,0:T(8,128)(2,1)S(1)}, u32[]{:S(2)}, u32[]{:S(2)}) collective-permute-start(bf16[256,2048]{1,0:T(8,128)(2,1)} %bitcast.19), channel_id=1, source_target_pairs={{6,8},{14,16},{22,24},{24,26},{26,28},{28,30},{7,9},{15,17},{23,25... | collective-permute-start | bytes 3145736 | tf_op jit(solution)/shard_map/ppermute | solution.py:234
  1.4 50.7 %collective-permute-start.1 = (bf16[256,2048]{1,0:T(8,128)(2,1)}, bf16[256,2048]{1,0:T(8,128)(2,1)S(1)}, u32[]{:S(2)}, u32[]{:S(2)}) collective-permute-start(bf16[256,2048]{1,0:T(8,128)(2,1)} %bitcast.20), channel_id=1, source_target_pairs={{0,2},{2,4},{4,6},{8,10},{10,12},{12,14},{16,18},{18,20},{20,22},{... | collective-permute-start | bytes 3145736 | tf_op jit(solution)/shard_map/ppermute | solution.py:234
  4.8 71.9 %collective-permute-start.8 = (bf16[256,2048]{1,0:T(8,128)(2,1)}, bf16[256,2048]{1,0:T(8,128)(2,1)S(1)}, u32[]{:S(2)}, u32[]{:S(2)}) collective-permute-start(bf16[256,2048]{1,0:T(8,128)(2,1)} %bitcast.17), channel_id=1, source_target_pairs={{2,0},{4,2},{6,4},{8,6},{10,8},{12,10},{14,12},{16,14},{18,16},{20... | collective-permute-start | bytes 3145736 | tf_op jit(solution)/shard_map/ppermute | solution.py:234
  7.3 70.8 %collective-permute-start.10 = (bf16[256,2048]{1,0:T(8,128)(2,1)}, bf16[256,2048]{1,0:T(8,128)(2,1)S(1)}, u32[]{:S(2)}, u32[]{:S(2)}) collective-permute-start(bf16[256,2048]{1,0:T(8,128)(2,1)} %bitcast.18), channel_id=1, source_target_pairs={{0,30},{2,28},{4,26},{6,24},{8,22},{10,20},{12,18},{14,16},{16,14}... | collective-permute-start | bytes 3145736 | tf_op jit(solution)/shard_map/ppermute | solution.py:234
  52.1 1.2 copy-start.2
  53.3 25.4 %copy-start = (bf16[1,4096,512]{2,1,0:T(8,128)(2,1)S(1)}, bf16[1,4096,512]{2,1,0:T(8,128)(2,1)}, u32[]{:S(2)}) copy-start(bf16[1,4096,512]{2,1,0:T(8,128)(2,1)} %param.15) | copy-start | bytes 12582916
  53.4 25.3 %copy-start.4 = (bf16[1,4096,256]{2,1,0:T(8,128)(2,1)S(1)}, bf16[1,4096,256]{2,1,0:T(8,128)(2,1)}, u32[]{:S(2)}) copy-start(bf16[1,4096,256]{2,1,0:T(8,128)(2,1)} %param.16) | copy-start | bytes 6291460
  53.4 28.9 %collective-permute-start.2 = (bf16[256,2048]{1,0:T(8,128)(2,1)S(1)}, bf16[256,2048]{1,0:T(8,128)(2,1)S(1)}, u32[]{:S(2)}, u32[]{:S(2)}) collective-permute-start(bf16[256,2048]{1,0:T(8,128)(2,1)S(1)} %shard_map.112.refs_0_), channel_id=1, source_target_pairs={{0,1},{1,0},{2,3},{3,2},{4,5},{5,4},{6,7},{7,6},{8,9},{9,8},{10,11... | collective-permute-start | bytes 3145736 | tf_op jit(solution)/shard_map/ppermute | solution.py:22
  76.7 1.2 copy-start.5
  78.0 0.7 copy-start.6
  78.0 9.7 %collective-permute-start.9 = (bf16[256,2048]{1,0:T(8,128)(2,1)S(1)}, bf16[256,2048]{1,0:T(8,128)(2,1)S(1)}, u32[]{:S(2)}, u32[]{:S(2)}) collective-permute-start(bf16[256,2048]{1,0:T(8,128)(2,1)S(1)} %shard_map.115.refs_0_), channel_id=1, source_target_pairs={{0,1},{1,0},{2,3},{3,2},{4,5},{5,4},{6,7},{7,6},{8,9},{9,8},{10,11... | collective-permute-start | bytes 3145736 | tf_op jit(solution)/shard_map/ppermute | solution.py:22
  78.1 9.6 %collective-permute-start.11 = (bf16[256,2048]{1,0:T(8,128)(2,1)S(1)}, bf16[256,2048]{1,0:T(8,128)(2,1)S(1)}, u32[]{:S(2)}, u32[]{:S(2)}) collective-permute-start(bf16[256,2048]{1,0:T(8,128)(2,1)S(1)} %collective-permute-done.10.refs_2_), channel_id=1, source_target_pairs={{0,1},{1,0},{2,3},{3,2},{4,5},{5,4},{6,7},{7,6},{8,9},{9,8},{10,11... | collective-permute-start | bytes 3145736 | tf_op jit(solution)/shard_map/ppermute | solution.py:22
  78.6 3.6 %collective-permute-start.3 = (bf16[1,2048]{1,0:T(2,128)(2,1)S(1)}, bf16[1,2048]{1,0:T(2,128)(2,1)S(1)}, u32[]{:S(2)}, u32[]{:S(2)}) collective-permute-start(bf16[1,2048]{1,0:T(2,128)(2,1)S(1)} %copy-done.6), channel_id=1, source_target_pairs={{0,1},{1,0},{2,3},{3,2},{4,5},{5,4},{6,7},{7,6},{8,9},{9,8},{10,11... | collective-permute-start | bytes 12296 | tf_op jit(solution)/shard_map/ppermute | solution.py:22
  78.7 2.2 %copy-start.1 = (bf16[1,512,4096]{2,1,0:T(8,128)(2,1)S(1)}, bf16[1,512,4096]{2,1,0:T(8,128)(2,1)}, u32[]{:S(2)}) copy-start(bf16[1,512,4096]{2,1,0:T(8,128)(2,1)} %param.17) | copy-start | bytes 12582916
  87.5 10.1 %copy-start.7 = (bf16[1,256,2048]{2,1,0:T(8,128)(2,1)S(1)}, bf16[1,256,2048]{2,1,0:T(8,128)(2,1)}, u32[]{:S(2)}) copy-start(bf16[1,256,2048]{2,1,0:T(8,128)(2,1)} %param.10) | copy-start | bytes 3145732
  87.5 15.3 %collective-permute-start.4 = (bf16[256,2048]{1,0:T(8,128)(2,1)S(1)}, bf16[256,2048]{1,0:T(8,128)(2,1)S(1)}, u32[]{:S(2)}, u32[]{:S(2)}) collective-permute-start(bf16[256,2048]{1,0:T(8,128)(2,1)S(1)} %get-tuple-element.18), channel_id=1, source_target_pairs={{0,1},{1,0},{2,3},{3,2},{4,5},{5,4},{6,7},{7,6},{8,9},{9,8},{10,11... | collective-permute-start | bytes 3145736 | tf_op jit(solution)/shard_map/ppermute | solution.py:22
  97.1 7.3 %collective-permute-start.12 = (bf16[256,2048]{1,0:T(8,128)(2,1)S(1)}, bf16[256,2048]{1,0:T(8,128)(2,1)S(1)}, u32[]{:S(2)}, u32[]{:S(2)}) collective-permute-start(bf16[256,2048]{1,0:T(8,128)(2,1)S(1)} %get-tuple-element.22), channel_id=1, source_target_pairs={{0,1},{1,0},{2,3},{3,2},{4,5},{5,4},{6,7},{7,6},{8,9},{9,8},{10,11... | collective-permute-start | bytes 3145736 | tf_op jit(solution)/shard_map/ppermute | solution.py:22
  97.5 4.5 %collective-permute-start.13 = (f32[256,128]{1,0:T(8,128)S(1)}, f32[256,128]{1,0:T(8,128)S(1)}, u32[]{:S(2)}, u32[]{:S(2)}) collective-permute-start(f32[256,128]{1,0:T(8,128)S(1)} %get-tuple-element.23), channel_id=1, source_target_pairs={{0,1},{1,0},{2,3},{3,2},{4,5},{5,4},{6,7},{7,6},{8,9},{9,8},{10,11... | collective-permute-start | bytes 393224 | tf_op jit(solution)/shard_map/ppermute | solution.py:22
  97.6 8.6 %collective-permute-start.6 = (bf16[256,2048]{1,0:T(8,128)(2,1)S(1)}, bf16[256,2048]{1,0:T(8,128)(2,1)S(1)}, u32[]{:S(2)}, u32[]{:S(2)}) collective-permute-start(bf16[256,2048]{1,0:T(8,128)(2,1)S(1)} %bitcast.21), channel_id=1, source_target_pairs={{6,22},{7,23}} | collective-permute-start | bytes 3145736 | tf_op jit(solution)/shard_map/ppermute | solution.py:234
  98.4 49.8 %collective-permute-start.7 = (bf16[256,2048]{1,0:T(8,128)(2,1)S(1)}, bf16[256,2048]{1,0:T(8,128)(2,1)S(1)}, u32[]{:S(2)}, u32[]{:S(2)}) collective-permute-start(bf16[256,2048]{1,0:T(8,128)(2,1)S(1)} %bitcast.22), channel_id=1, source_target_pairs={{0,28},{2,26},{4,24},{8,20},{10,18},{12,16},{14,14},{16,12},{18,10... | collective-permute-start | bytes 3145736 | tf_op jit(solution)/shard_map/ppermute | solution.py:234
  102.0 46.1 %collective-permute-start.5 = (bf16[256,2048]{1,0:T(8,128)(2,1)S(1)}, bf16[256,2048]{1,0:T(8,128)(2,1)S(1)}, u32[]{:S(2)}, u32[]{:S(2)}) collective-permute-start(bf16[256,2048]{1,0:T(8,128)(2,1)S(1)} %collective-permute-done.refs_1_), channel_id=1, source_target_pairs={{26,4},{28,2},{30,0},{27,5},{29,3},{31,1}} | collective-permute-start | bytes 3145736 | tf_op jit(solution)/shard_map/ppermute | solution.py:234
  104.4 43.8 %copy-start.3 = (bf16[256,2048]{1,0:T(8,128)(2,1)S(1)}, bf16[256,2048]{1,0:T(8,128)(2,1)}, u32[]{:S(2)}) copy-start(bf16[256,2048]{1,0:T(8,128)(2,1)} %last) | copy-start | bytes 3145732

commit v3 on v2

--- a/solution.py
+++ b/solution.py
@@ -186,18 +186,28 @@
             copy.wait()
 
 
-def merge_kernel(count, block, relayed, alone, direct, last, out, sem):
+def merge_kernel(count, block, relayed, rest, alone, direct, last, out, sem):
     place, sections = lax.axis_index("section"), lax.axis_size("section")
     is_last = place == sections - 1
     is_alone = place == sections - 1 - block
     is_relayed = place < block - 1
     is_direct = jnp.logical_not(is_last | is_alone | is_relayed)
-    chosen = ((is_relayed, relayed), (is_alone, alone), (is_direct, direct), (is_last, last))
-    for here, source in chosen:
+
+    @pl.when(is_relayed)
+    def _():
+        cut, seq = relayed.shape[0], out.shape[0]
+        upper = pltpu.make_async_copy(relayed, out.at[pl.ds(0, cut), :], sem.at[0])
+        lower = pltpu.make_async_copy(rest, out.at[pl.ds(cut, seq - cut), :], sem.at[1])
+        upper.start()
+        lower.start()
+        upper.wait()
+        lower.wait()
+
+    for here, source in ((is_alone, alone), (is_direct, direct), (is_last, last)):
 
         @pl.when(here)
         def _():
-            copy = pltpu.make_async_copy(source, out, sem)
+            copy = pltpu.make_async_copy(source, out, sem.at[0])
             copy.start()
             copy.wait()
 
@@ -243,7 +253,9 @@
     later = send(held, [(s, t) for s, t in up if not early(t)])
     evicted = send(held, [(s, sections - 2 - s) for s in range(high) if s != block - 1])
     alone = send(held, [(block - 1, sections - 1 - block)])
-    relayed = send(soon, [(s, sections - 1 - s) for s in range(high + 1, sections)])
+    cut = seq - seq // 16
+    relayed = send(soon[:cut], [(s, sections - 1 - s) for s in range(high + 1, sections)])
+    rest = send(held[cut:], [(s, sections - 2 - s) for s in range(high, sections - 1)])
     gains = gathered(norm_gain, "tensor")
 
     normed = pltpu.VMEM((seq, model), BF16)
@@ -305,8 +317,8 @@
     last, _ = lax.optimization_barrier((embedded, (result, section_out)))
     (evicted,) = call(
         merge_kernel, count, block,
-        [relayed, alone, evicted, last], [shape((seq, width), BF16)],
-        [pltpu.SemaphoreType.DMA], 0, 4 * seq * width, far_out=1,
+        [relayed, rest, alone, evicted, last], [shape((seq, width), BF16)],
+        [pltpu.SemaphoreType.DMA((2,))], 0, 4 * seq * width, far_out=1,
     )
     return section_out[None], evicted[None], result[None]
 

time: 149 us -> 136 us (0.913)
  the two profiles are of different devices: /device:TPU:10 before, /device:TPU:0 now
where the time goes in v3:
time: 136 us
  waiting for transfers between devices  85.5 us (63%)
  starting transfers between devices  23.8 us (18%)
  Pallas kernels  16.4 us (12%)
  local copies, waits for them, and re-layouts  5.56 us (4%)
  other arithmetic  3.59 us (3%)
    ppermute x8, waiting for transfers between devices, send(): return lax.ppermute(value, 'section', pairs)  84.9 us
    ppermute x8, starting transfers between devices, send(): return lax.ppermute(value, 'section', pairs)  22.3 us
    pallas_call x6, Pallas kernels, call(): pl.pallas_call(functools.partial(kernel, count, heads), out_shape=out_sha...  16.4 us
    unnamed x16, local copies, waits for them, and re-layouts  5.49 us
  transfers between devices with their start and end apart: 15, of which 5 were waited for; matrix products, arithmetic and copies ran while one was open for 3% of the time, Pallas kernels for 11%

profile of v3, /device:TPU:0, one launch (start us, length us, event | category | flops | bytes accessed | tf_op | source)
XLA Modules:
  0.0 135.7 jit_solution(15863768608699651705)
XLA Ops:
  0.6 0.7 collective-permute-start
  1.4 4.9 %collective-permute-start.1 = (bf16[256,2048]{1,0:T(8,128)(2,1)}, bf16[256,2048]{1,0:T(8,128)(2,1)S(1)}, u32[]{:S(2)}, u32[]{:S(2)}) collective-permute-start(bf16[256,2048]{1,0:T(8,128)(2,1)} %bitcast.20), channel_id=1, source_target_pairs={{0,2},{2,4},{4,6},{8,10},{10,12},{12,14},{16,18},{18,20},{20,22},{... | collective-permute-start | bytes 3145736 | tf_op jit(solution)/shard_map/ppermute | solution.py:244
  6.3 1.3 collective-permute-start.9
  7.6 6.7 %collective-permute-start.11 = (bf16[256,2048]{1,0:T(8,128)(2,1)}, bf16[256,2048]{1,0:T(8,128)(2,1)S(1)}, u32[]{:S(2)}, u32[]{:S(2)}) collective-permute-start(bf16[256,2048]{1,0:T(8,128)(2,1)} %bitcast.24), channel_id=1, source_target_pairs={{0,30},{2,28},{4,26},{6,24},{8,22},{10,20},{12,18},{14,16},{16,14}... | collective-permute-start | bytes 3145736 | tf_op jit(solution)/shard_map/ppermute | solution.py:244
  14.3 59.6 %collective-permute-done.1.refs_2_ = bf16[256,2048]{1,0:T(8,128)(2,1)S(1)} collective-permute-done((bf16[256,2048]{1,0:T(8,128)(2,1)}, bf16[256,2048]{1,0:T(8,128)(2,1)S(1)}, u32[]{:S(2)}, u32[]{:S(2)}) %collective-permute-start.1) | collective-permute-done | bytes 1048608 | tf_op jit(solution)/shard_map/ppermute | solution.py:244
  73.9 1.2 copy-done.2
  75.3 0.4 collective-permute-done.9.refs_1_
  75.7 1.5 %copy-done.5 = bf16[256,2048]{1,0:T(8,128)(2,1)S(1)} copy-done((bf16[256,2048]{1,0:T(8,128)(2,1)S(1)}, bf16[256,2048]{1,0:T(8,128)(2,1)}, u32[]{:S(2)}) %copy-start.5) | copy-done | bytes 1048600
  77.5 0.5 collective-permute-start.12
  78.0 0.7 collective-permute-start.7
  78.8 2.2 %copy-done.1 = bf16[1,512,4096]{2,1,0:T(8,128)(2,1)S(1)} copy-done((bf16[1,512,4096]{2,1,0:T(8,128)(2,1)S(1)}, bf16[1,512,4096]{2,1,0:T(8,128)(2,1)}, u32[]{:S(2)}) %copy-start.1) | copy-done | bytes 4194328
  81.0 0.7 shard_map.113
  81.7 0.5 copy-done.7
  82.2 5.4 %collective-permute-start.8 = (bf16[256,2048]{1,0:T(8,128)(2,1)S(1)}, bf16[256,2048]{1,0:T(8,128)(2,1)S(1)}, u32[]{:S(2)}, u32[]{:S(2)}) collective-permute-start(bf16[256,2048]{1,0:T(8,128)(2,1)S(1)} %bitcast.22), channel_id=1, source_target_pairs={{0,28},{2,26},{4,24},{8,20},{10,18},{12,16},{14,14},{16,12},{18,10... | collective-permute-start | bytes 3145736 | tf_op jit(solution)/shard_map/ppermute | solution.py:244
  87.6 5.2 %shard_map.114 = (bf16[256,2048]{1,0:T(8,128)(2,1)S(1)}, bf16[256,2048]{1,0:T(8,128)(2,1)S(1)}) custom-call(bf16[256,2048]{1,0:T(8,128)(2,1)S(1)} %shard_map.112.refs_0_, bf16[256,2048]{1,0:T(8,128)(2,1)S(1)} %collective-permute-done.2.refs_1_, bf16[1,2048]{1,0:T(2,128)(2,1)S(1)} %copy-done.6, bf16[1,2048]{1,0:T(2,128)(2,1)S(1)} %collective-permute-done.3.refs_3_.refs_5_, ...), custom_call_target="tpu_custom_call" | custom-call | flops 2684354560 | bytes 10485760 | tf_op jit(solution)/shard_map/pallas_call | solution.py:216
  93.1 9.3 %shard_map.116 = (bf16[256,2048]{1,0:T(8,128)(2,1)S(1)}, bf16[256,2048]{1,0:T(8,128)(2,1)S(1)}, f32[256,128]{1,0:T(8,128)S(1)}, f32[256,128]{1,0:T(8,128)S(1)}) custom-call(bf16[256,2048]{1,0:T(8,128)(2,1)S(1)} %shard_map.115.refs_0_, bf16[256,2048]{1,0:T(8,128)(2,1)S(1)} %collective-permute-done.10.refs_1_, ...), custom_call_target="tpu_custom_call" | custom-call | flops 4294967296 | bytes 10485760 | tf_op jit(solution)/shard_map/pallas_call | solution.py:216
  103.2 0.6 collective-permute-done.14
  103.8 1.3 collective-permute-start.6
  105.2 1.3 collective-permute-start.5
  106.5 1.5 %add_convert_fusion = bf16[256,2048]{1,0:T(8,128)(2,1)} fusion(bf16[256,2048]{1,0:T(8,128)(2,1)S(1)} %collective-permute-done.4, bf16[256,2048]{1,0:T(8,128)(2,1)S(1)} %get-tuple-element.17, bf16[256,2048]{1,0:T(8,128)(2,1)S(1)} %shard_map.112.refs_0_), kind=kLoop, calls=%fused_computation.1 | loop fusion | flops 3145728 | bytes 4194304 | tf_op jit(solution)/shard_map/convert_element_type | solution.py:307
  108.0 1.8 %subtract_convert_fusion = bf16[256,2048]{1,0:T(8,128)(2,1)} fusion(bf16[256,2048]{1,0:T(8,128)(2,1)S(1)} %collective-permute-done.11.refs_2_, bf16[256,2048]{1,0:T(8,128)(2,1)S(1)} %collective-permute-done.13, bf16[256,2048]{1,0:T(8,128)(2,1)S(1)} %get-tuple-element.21, bf16[256,2048]{1,0:T(8,128)(2,1)S(1)} %shard_map.115.refs_0_, f32[256]{0:T(256)S(1)} %fusion.2, ...), kind=kLoop, calls=%fused_computation | loop fusion | flops 6291456 | bytes 5254144 | tf_op jit(solution)/shard_map/convert_element_type | solution.py:316
  109.8 3.0 %collective-permute-done.6.rest = bf16[16,2048]{1,0:T(8,128)(2,1)S(1)} collective-permute-done((bf16[16,2048]{1,0:T(8,128)(2,1)S(1)}, bf16[16,2048]{1,0:T(8,128)(2,1)S(1)}, u32[]{:S(2)}, u32[]{:S(2)}) %collective-permute-start.6) | collective-permute-done | bytes 65568 | tf_op jit(solution)/shard_map/ppermute | solution.py:244
  112.8 21.9 %collective-permute-done.5.relayed = bf16[240,2048]{1,0:T(8,128)(2,1)S(1)} collective-permute-done((bf16[240,2048]{1,0:T(8,128)(2,1)S(1)}, bf16[240,2048]{1,0:T(8,128)(2,1)S(1)}, u32[]{:S(2)}, u32[]{:S(2)}) %collective-permute-start.5) | collective-permute-done | bytes 983072 | tf_op jit(solution)/shard_map/ppermute | solution.py:244
  134.7 1.0 shard_map.117
  (35 shorter events, 1.6 us)
Async XLA Ops:
  0.6 13.7 %collective-permute-start = (bf16[256,2048]{1,0:T(8,128)(2,1)}, bf16[256,2048]{1,0:T(8,128)(2,1)S(1)}, u32[]{:S(2)}, u32[]{:S(2)}) collective-permute-start(bf16[256,2048]{1,0:T(8,128)(2,1)} %bitcast.19), channel_id=1, source_target_pairs={{6,8},{14,16},{22,24},{24,26},{26,28},{28,30},{7,9},{15,17},{23,25... | collective-permute-start | bytes 3145736 | tf_op jit(solution)/shard_map/ppermute | solution.py:244
  1.4 72.5 %collective-permute-start.1 = (bf16[256,2048]{1,0:T(8,128)(2,1)}, bf16[256,2048]{1,0:T(8,128)(2,1)S(1)}, u32[]{:S(2)}, u32[]{:S(2)}) collective-permute-start(bf16[256,2048]{1,0:T(8,128)(2,1)} %bitcast.20), channel_id=1, source_target_pairs={{0,2},{2,4},{4,6},{8,10},{10,12},{12,14},{16,18},{18,20},{20,22},{... | collective-permute-start | bytes 3145736 | tf_op jit(solution)/shard_map/ppermute | solution.py:244
  6.3 69.4 %collective-permute-start.9 = (bf16[256,2048]{1,0:T(8,128)(2,1)}, bf16[256,2048]{1,0:T(8,128)(2,1)S(1)}, u32[]{:S(2)}, u32[]{:S(2)}) collective-permute-start(bf16[256,2048]{1,0:T(8,128)(2,1)} %bitcast.23), channel_id=1, source_target_pairs={{2,0},{4,2},{6,4},{8,6},{10,8},{12,10},{14,12},{16,14},{18,16},{20... | collective-permute-start | bytes 3145736 | tf_op jit(solution)/shard_map/ppermute | solution.py:244
  7.6 69.8 %collective-permute-start.11 = (bf16[256,2048]{1,0:T(8,128)(2,1)}, bf16[256,2048]{1,0:T(8,128)(2,1)S(1)}, u32[]{:S(2)}, u32[]{:S(2)}) collective-permute-start(bf16[256,2048]{1,0:T(8,128)(2,1)} %bitcast.24), channel_id=1, source_target_pairs={{0,30},{2,28},{4,26},{6,24},{8,22},{10,20},{12,18},{14,16},{16,14}... | collective-permute-start | bytes 3145736 | tf_op jit(solution)/shard_map/ppermute | solution.py:244
  73.9 1.2 copy-start.2
  75.1 3.6 %copy-start = (bf16[1,4096,512]{2,1,0:T(8,128)(2,1)S(1)}, bf16[1,4096,512]{2,1,0:T(8,128)(2,1)}, u32[]{:S(2)}) copy-start(bf16[1,4096,512]{2,1,0:T(8,128)(2,1)} %param.15) | copy-start | bytes 12582916
  75.2 3.5 %copy-start.4 = (bf16[1,4096,256]{2,1,0:T(8,128)(2,1)S(1)}, bf16[1,4096,256]{2,1,0:T(8,128)(2,1)}, u32[]{:S(2)}) copy-start(bf16[1,4096,256]{2,1,0:T(8,128)(2,1)} %param.16) | copy-start | bytes 6291460
  75.2 12.3 %collective-permute-start.2 = (bf16[256,2048]{1,0:T(8,128)(2,1)S(1)}, bf16[256,2048]{1,0:T(8,128)(2,1)S(1)}, u32[]{:S(2)}, u32[]{:S(2)}) collective-permute-start(bf16[256,2048]{1,0:T(8,128)(2,1)S(1)} %shard_map.112.refs_0_), channel_id=1, source_target_pairs={{0,1},{1,0},{2,3},{3,2},{4,5},{5,4},{6,7},{7,6},{8,9},{9,8},{10,11... | collective-permute-start | bytes 3145736 | tf_op jit(solution)/shard_map/ppermute | solution.py:22
  75.7 1.5 %copy-start.5 = (bf16[256,2048]{1,0:T(8,128)(2,1)S(1)}, bf16[256,2048]{1,0:T(8,128)(2,1)}, u32[]{:S(2)}) copy-start(bf16[256,2048]{1,0:T(8,128)(2,1)} %refs_0_.3) | copy-start | bytes 3145732
  77.3 0.7 copy-start.6
  77.4 15.7 %collective-permute-start.10 = (bf16[256,2048]{1,0:T(8,128)(2,1)S(1)}, bf16[256,2048]{1,0:T(8,128)(2,1)S(1)}, u32[]{:S(2)}, u32[]{:S(2)}) collective-permute-start(bf16[256,2048]{1,0:T(8,128)(2,1)S(1)} %shard_map.115.refs_0_), channel_id=1, source_target_pairs={{0,1},{1,0},{2,3},{3,2},{4,5},{5,4},{6,7},{7,6},{8,9},{9,8},{10,11... | collective-permute-start | bytes 3145736 | tf_op jit(solution)/shard_map/ppermute | solution.py:22
  77.5 15.6 %collective-permute-start.12 = (bf16[256,2048]{1,0:T(8,128)(2,1)S(1)}, bf16[256,2048]{1,0:T(8,128)(2,1)S(1)}, u32[]{:S(2)}, u32[]{:S(2)}) collective-permute-start(bf16[256,2048]{1,0:T(8,128)(2,1)S(1)} %collective-permute-done.11.refs_2_), channel_id=1, source_target_pairs={{0,1},{1,0},{2,3},{3,2},{4,5},{5,4},{6,7},{7,6},{8,9},{9,8},{10,11... | collective-permute-start | bytes 3145736 | tf_op jit(solution)/shard_map/ppermute | solution.py:22
  78.0 3.7 %collective-permute-start.3 = (bf16[1,2048]{1,0:T(2,128)(2,1)S(1)}, bf16[1,2048]{1,0:T(2,128)(2,1)S(1)}, u32[]{:S(2)}, u32[]{:S(2)}) collective-permute-start(bf16[1,2048]{1,0:T(2,128)(2,1)S(1)} %copy-done.6), channel_id=1, source_target_pairs={{0,1},{1,0},{2,3},{3,2},{4,5},{5,4},{6,7},{7,6},{8,9},{9,8},{10,11... | collective-permute-start | bytes 12296 | tf_op jit(solution)/shard_map/ppermute | solution.py:22
  78.0 34.8 %collective-permute-start.7 = (bf16[256,2048]{1,0:T(8,128)(2,1)}, bf16[256,2048]{1,0:T(8,128)(2,1)S(1)}, u32[]{:S(2)}, u32[]{:S(2)}) collective-permute-start(bf16[256,2048]{1,0:T(8,128)(2,1)} %bitcast.21), channel_id=1, source_target_pairs={{6,22},{7,23}} | collective-permute-start | bytes 3145736 | tf_op jit(solution)/shard_map/ppermute | solution.py:244
  78.8 2.2 %copy-start.1 = (bf16[1,512,4096]{2,1,0:T(8,128)(2,1)S(1)}, bf16[1,512,4096]{2,1,0:T(8,128)(2,1)}, u32[]{:S(2)}) copy-start(bf16[1,512,4096]{2,1,0:T(8,128)(2,1)} %param.17) | copy-start | bytes 12582916
  81.0 1.2 copy-start.7
  82.2 30.6 %collective-permute-start.8 = (bf16[256,2048]{1,0:T(8,128)(2,1)S(1)}, bf16[256,2048]{1,0:T(8,128)(2,1)S(1)}, u32[]{:S(2)}, u32[]{:S(2)}) collective-permute-start(bf16[256,2048]{1,0:T(8,128)(2,1)S(1)} %bitcast.22), channel_id=1, source_target_pairs={{0,28},{2,26},{4,24},{8,20},{10,18},{12,16},{14,14},{16,12},{18,10... | collective-permute-start | bytes 3145736 | tf_op jit(solution)/shard_map/ppermute | solution.py:244
  92.8 12.4 %collective-permute-start.4 = (bf16[256,2048]{1,0:T(8,128)(2,1)S(1)}, bf16[256,2048]{1,0:T(8,128)(2,1)S(1)}, u32[]{:S(2)}, u32[]{:S(2)}) collective-permute-start(bf16[256,2048]{1,0:T(8,128)(2,1)S(1)} %get-tuple-element.18), channel_id=1, source_target_pairs={{0,1},{1,0},{2,3},{3,2},{4,5},{5,4},{6,7},{7,6},{8,9},{9,8},{10,11... | collective-permute-start | bytes 3145736 | tf_op jit(solution)/shard_map/ppermute | solution.py:22
  102.4 1.4 %collective-permute-start.14 = (f32[256,128]{1,0:T(8,128)S(1)}, f32[256,128]{1,0:T(8,128)S(1)}, u32[]{:S(2)}, u32[]{:S(2)}) collective-permute-start(f32[256,128]{1,0:T(8,128)S(1)} %get-tuple-element.23), channel_id=1, source_target_pairs={{0,1},{1,0},{2,3},{3,2},{4,5},{5,4},{6,7},{7,6},{8,9},{9,8},{10,11... | collective-permute-start | bytes 393224 | tf_op jit(solution)/shard_map/ppermute | solution.py:22
  102.8 5.2 %collective-permute-start.13 = (bf16[256,2048]{1,0:T(8,128)(2,1)S(1)}, bf16[256,2048]{1,0:T(8,128)(2,1)S(1)}, u32[]{:S(2)}, u32[]{:S(2)}) collective-permute-start(bf16[256,2048]{1,0:T(8,128)(2,1)S(1)} %get-tuple-element.22), channel_id=1, source_target_pairs={{0,1},{1,0},{2,3},{3,2},{4,5},{5,4},{6,7},{7,6},{8,9},{9,8},{10,11... | collective-permute-start | bytes 3145736 | tf_op jit(solution)/shard_map/ppermute | solution.py:22
  103.8 9.0 %collective-permute-start.6 = (bf16[16,2048]{1,0:T(8,128)(2,1)S(1)}, bf16[16,2048]{1,0:T(8,128)(2,1)S(1)}, u32[]{:S(2)}, u32[]{:S(2)}) collective-permute-start(bf16[16,2048]{1,0:T(8,128)(2,1)S(1)} %slice_bitcast_fusion), channel_id=1, source_target_pairs={{24,4},{26,2},{28,0},{25,5},{27,3},{29,1}} | collective-permute-start | bytes 196616 | tf_op jit(solution)/shard_map/ppermute | solution.py:244
  105.2 29.5 %collective-permute-start.5 = (bf16[240,2048]{1,0:T(8,128)(2,1)S(1)}, bf16[240,2048]{1,0:T(8,128)(2,1)S(1)}, u32[]{:S(2)}, u32[]{:S(2)}) collective-permute-start(bf16[240,2048]{1,0:T(8,128)(2,1)S(1)} %slice.20), channel_id=1, source_target_pairs={{26,4},{28,2},{30,0},{27,5},{29,3},{31,1}} | collective-permute-start | bytes 2949128 | tf_op jit(solution)/shard_map/ppermute | solution.py:244
  108.0 26.7 %copy-start.3 = (bf16[256,2048]{1,0:T(8,128)(2,1)S(1)}, bf16[256,2048]{1,0:T(8,128)(2,1)}, u32[]{:S(2)}) copy-start(bf16[256,2048]{1,0:T(8,128)(2,1)} %last) | copy-start | bytes 3145732
